TPU v7x, 256 devices: a whole 4x4x8 slice. The times are simulated.
256 devices in a mesh: dp: 8 (over x, core), context: 32 (over z, y).
Axes of the slice: x: 4, y: 4, z: 8, core: 2. Of those that a mesh axis runs over, the one named last changes fastest.
Arguments:
- inputs: bfloat16 [8, 16384, 1024], P('dp', 'context'), may hold values from -6 to 6
- step_size: float32 [8, 16384], P('dp', 'context'), may hold values from 0.25 to 16387
- decay_rate: float32 [256], replicated, may hold values from 1.2207031e-05 to 0.125
- frequency: float32 [256], replicated, may hold values from -0.5 to 0.5
- input_proj: bfloat16 [1024, 512], replicated, may hold values from -0.1875 to 0.1875
- output_proj: bfloat16 [1024, 512], replicated, may hold values from -0.25 to 0.25
- skip_gain: float32 [1024], replicated, may hold values from 0.25 to 1.75
- cotangent: bfloat16 [8, 16384, 1024], P('dp', 'context'), may hold values from -6 to 6
Outputs:
- outputs: bfloat16 [8, 16384, 1024], P('dp', 'context')
- input_grad: bfloat16 [8, 16384, 1024], P('dp', 'context')
- input_proj_grad: float32 [1024, 512], P('context')
- output_proj_grad: float32 [1024, 512], P('context')
All inputs are finite; a program needn't handle non-finite values.
Results may differ from a plain program's by a relative error of at most 0.0036.
Values sent between devices are 32-bit elements; how exact they have to be, the bound alone decides.
A program may use at most 64 MiB of HBM per device.

v0:
```python
import jax
import jax.numpy as jnp
from jax import lax
from jax.sharding import PartitionSpec as P


def prefix(x, axis, combine, identity, reverse):
    peers, place = (lax.axis_size(axis), lax.axis_index(axis))
    everything = jax.tree.map(lambda part: lax.all_gather(part, axis), x)
    start = jax.tree.map(
        lambda part, zero: jnp.broadcast_to(jnp.asarray(zero, part.dtype), part.shape), x, identity
    )

    def lap(k, before):
        at = peers - 1 - k if reverse else k
        reached = at > place if reverse else at < place
        new = combine(before, jax.tree.map(lambda part: part[at], everything))
        return jax.tree.map(lambda a, b: jnp.where(reached, a, b), new, before)

    return lax.fori_loop(0, peers, lap, start)


def complex_combine(earlier_pair, later_pair):
    early_are, early_aim, early_bre, early_bim = earlier_pair
    later_are, later_aim, later_bre, later_bim = later_pair
    return (
        later_are * early_are - later_aim * early_aim,
        later_are * early_aim + later_aim * early_are,
        later_are * early_bre - later_aim * early_bim + later_bre,
        later_are * early_bim + later_aim * early_bre + later_bim,
    )


def on_device(
    inputs, step_size, decay_rate, frequency, input_proj, output_proj, skip_gain, cotangent
):
    batch_count, row_count, model_width = inputs.shape
    state_count = decay_rate.shape[0]
    damping = jnp.exp(-step_size[:, :, None] * decay_rate)
    phase_turn = step_size[:, :, None] * frequency
    lam_re = damping * jnp.cos(phase_turn)
    lam_im = damping * jnp.sin(phase_turn)
    norm_gain = jnp.sqrt(-jnp.expm1(-2.0 * decay_rate))
    pair_gain = jnp.concatenate([norm_gain, norm_gain])
    flat_in = inputs.reshape(batch_count * row_count, model_width)
    flat_cot = cotangent.reshape(batch_count * row_count, model_width)
    drive_term = (
        jnp.dot(flat_in, input_proj, preferred_element_type=jnp.float32).reshape(
            batch_count, row_count, 2 * state_count
        )
        * pair_gain
    )
    local_fwd = lax.associative_scan(
        complex_combine,
        (lam_re, lam_im, drive_term[..., :state_count], drive_term[..., state_count:]),
        axis=1,
    )
    fwd_summary = (
        local_fwd[0][:, -1],
        local_fwd[1][:, -1],
        local_fwd[2][:, -1],
        local_fwd[3][:, -1],
    )
    adjoint_drive = jnp.dot(flat_cot, output_proj, preferred_element_type=jnp.float32).reshape(
        batch_count, row_count, 2 * state_count
    )
    next_re = jnp.concatenate([lam_re[:, 1:], jnp.ones_like(lam_re[:, :1])], axis=1)
    next_im = jnp.concatenate([-lam_im[:, 1:], jnp.zeros_like(lam_im[:, :1])], axis=1)
    local_back = lax.associative_scan(
        complex_combine,
        (next_re, next_im, adjoint_drive[..., :state_count], adjoint_drive[..., state_count:]),
        axis=1,
        reverse=True,
    )
    first_re = lam_re[:, 0]
    first_im = -lam_im[:, 0]
    back_summary = (
        first_re * local_back[0][:, 0] - first_im * local_back[1][:, 0],
        first_re * local_back[1][:, 0] + first_im * local_back[0][:, 0],
        first_re * local_back[2][:, 0] - first_im * local_back[3][:, 0],
        first_re * local_back[3][:, 0] + first_im * local_back[2][:, 0],
    )
    unit_pair = (
        jnp.ones_like(fwd_summary[0]),
        jnp.zeros_like(fwd_summary[0]),
        jnp.zeros_like(fwd_summary[0]),
        jnp.zeros_like(fwd_summary[0]),
    )
    fwd_carry = prefix(fwd_summary, "context", complex_combine, unit_pair, False)
    back_carry = prefix(back_summary, "context", complex_combine, unit_pair, True)
    carry_re, carry_im = (fwd_carry[2], fwd_carry[3])
    inflow_re, inflow_im = (back_carry[2], back_carry[3])
    state_re = local_fwd[2] + local_fwd[0] * carry_re[:, None] - local_fwd[1] * carry_im[:, None]
    state_im = local_fwd[3] + local_fwd[0] * carry_im[:, None] + local_fwd[1] * carry_re[:, None]
    back_re = (
        local_back[2] + local_back[0] * inflow_re[:, None] - local_back[1] * inflow_im[:, None]
    )
    back_im = (
        local_back[3] + local_back[0] * inflow_im[:, None] + local_back[1] * inflow_re[:, None]
    )
    last_contract = (((1,), (1,)), ((), ()))
    state_pairs = (
        jnp.concatenate([state_re, state_im], axis=-1)
        .astype(jnp.bfloat16)
        .reshape(batch_count * row_count, 2 * state_count)
    )
    mixed = lax.dot_general(
        state_pairs, output_proj, last_contract, preferred_element_type=jnp.float32
    ).reshape(batch_count, row_count, model_width)
    outputs = (mixed + skip_gain * inputs.astype(jnp.float32)).astype(jnp.bfloat16)
    adjoint_pairs = (
        (jnp.concatenate([back_re, back_im], axis=-1) * pair_gain)
        .astype(jnp.bfloat16)
        .reshape(batch_count * row_count, 2 * state_count)
    )
    back_in = lax.dot_general(
        adjoint_pairs, input_proj, last_contract, preferred_element_type=jnp.float32
    ).reshape(batch_count, row_count, model_width)
    input_grad = (back_in + skip_gain * cotangent.astype(jnp.float32)).astype(jnp.bfloat16)
    context_count = lax.axis_size("context")
    grad_scale = float(batch_count * row_count * lax.axis_size("dp") * context_count) ** (-0.5)
    token_contract = (((0,), (0,)), ((), ()))
    grad_in_part = lax.dot_general(
        flat_in, adjoint_pairs, token_contract, preferred_element_type=jnp.float32
    )
    grad_out_part = lax.dot_general(
        flat_cot, state_pairs, token_contract, preferred_element_type=jnp.float32
    )
    shares = lax.psum_scatter(
        jnp.concatenate([grad_in_part, grad_out_part], axis=1) * grad_scale,
        "context",
        scatter_dimension=0,
        tiled=True,
    )
    my_rows = lax.psum(shares, "dp")
    return (outputs, input_grad, my_rows[:, : 2 * state_count], my_rows[:, 2 * state_count :])


def solution(mesh):
    in_specs = (
        P("dp", "context", None),
        P("dp", "context"),
        P(),
        P(),
        P(),
        P(),
        P(),
        P("dp", "context", None),
    )
    out_specs = (
        P("dp", "context", None),
        P("dp", "context", None),
        P("context", None),
        P("context", None),
    )
    return jax.shard_map(
        on_device, mesh=mesh, in_specs=in_specs, out_specs=out_specs, check_vma=False
    )
```

profile of v0, /device:TPU:1, one launch (start us, length us, event | category | flops | bytes accessed | tf_op | source)
XLA Modules:
  0.0 1171.3 jit_solution(17357458822823251579)
XLA Ops:
  8.0 2.7 fusion.12
  29.8 2.9 slice.1317
  32.8 2.9 slice.1323
  37.0 3.0 slice.1333
  40.0 3.0 slice.1320
  43.0 3.0 slice.1326
  46.0 3.0 slice.1328
  223.5 3.0 slice.1453
  226.5 3.0 slice.1458
  229.6 3.0 slice.1496
  443.0 4.7 rev.19
  447.8 37.2 %all_gather.32 = f32[32,1,256]{2,1,0:T(1,128)S(1)} all-gather(f32[1,1,256]{2,1,0:T(1,128)} %get-tuple-element.448), channel_id=1, replica_groups=mesh['dp'=8,'context'=32] {'context'}, dimensions={0}, use_global_device_ids=true | all-gather | bytes 33792 | tf_op jit(solution)/shard_map/all_gather | solution.py:9
  485.0 32.2 %all_gather.33 = f32[32,1,256]{2,1,0:T(1,128)S(1)} all-gather(f32[1,1,256]{2,1,0:T(1,128)} %get-tuple-element.447), channel_id=1, replica_groups=mesh['dp'=8,'context'=32] {'context'}, dimensions={0}, use_global_device_ids=true | all-gather | bytes 33792 | tf_op jit(solution)/shard_map/all_gather | solution.py:9
  517.1 31.2 %all_gather.34 = f32[32,1,256]{2,1,0:T(1,128)S(1)} all-gather(f32[1,1,256]{2,1,0:T(1,128)} %get-tuple-element.446), channel_id=1, replica_groups=mesh['dp'=8,'context'=32] {'context'}, dimensions={0}, use_global_device_ids=true | all-gather | bytes 33792 | tf_op jit(solution)/shard_map/all_gather | solution.py:9
  548.4 32.6 %all_gather.35 = f32[32,1,256]{2,1,0:T(1,128)S(1)} all-gather(f32[1,1,256]{2,1,0:T(1,128)} %get-tuple-element.445), channel_id=1, replica_groups=mesh['dp'=8,'context'=32] {'context'}, dimensions={0}, use_global_device_ids=true | all-gather | bytes 33792 | tf_op jit(solution)/shard_map/all_gather | solution.py:9
  581.0 37.7 %while.35 = (s32[]{:T(128)}, f32[1,256]{1,0:T(1,128)}, f32[1,256]{1,0:T(1,128)}, s32[]{:T(128)}, f32[32,1,256]{2,1,0:T(1,128)S(1)}, /*index=5*/f32[32,1,256]{2,1...) while((s32[]{:T(128)}, f32[1,256]{1,0:T(1,128)}, ...), condition=%wide.region_3.4_spmd.clone, body=%wide.region_2.3_spmd.clone.sunk | while | flops 3080 | bytes 8379 | solution.py:20
  618.7 2.6 rev.17
  621.3 2.6 rev.16
  641.0 30.6 %all_gather.31 = f32[32,1,256]{2,1,0:T(1,128)S(1)} all-gather(f32[1,1,256]{2,1,0:T(1,128)S(1)} %slice_add_fusion.64), channel_id=1, replica_groups=mesh['dp'=8,'context'=32] {'context'}, dimensions={0}, use_global_device_ids=true | all-gather | bytes 33792 | tf_op jit(solution)/shard_map/all_gather | solution.py:9
  673.7 31.8 %all_gather.29 = f32[32,1,256]{2,1,0:T(1,128)S(1)} all-gather(f32[1,1,256]{2,1,0:T(1,128)S(1)} %slice_add_fusion.66), channel_id=1, replica_groups=mesh['dp'=8,'context'=32] {'context'}, dimensions={0}, use_global_device_ids=true | all-gather | bytes 33792 | tf_op jit(solution)/shard_map/all_gather | solution.py:9
  707.2 2.6 pad.510
  709.9 2.7 pad.511
  713.3 30.6 %all_gather.28 = f32[32,1,256]{2,1,0:T(1,128)S(1)} all-gather(f32[1,1,256]{2,1,0:T(1,128)S(1)} %slice_add_fusion.67), channel_id=1, replica_groups=mesh['dp'=8,'context'=32] {'context'}, dimensions={0}, use_global_device_ids=true | all-gather | bytes 33792 | tf_op jit(solution)/shard_map/all_gather | solution.py:9
  743.9 2.6 pad.477
  747.2 2.6 pad.476
  750.5 32.2 %all_gather.30 = f32[32,1,256]{2,1,0:T(1,128)S(1)} all-gather(f32[1,1,256]{2,1,0:T(1,128)S(1)} %slice_add_fusion.65), channel_id=1, replica_groups=mesh['dp'=8,'context'=32] {'context'}, dimensions={0}, use_global_device_ids=true | all-gather | bytes 33792 | tf_op jit(solution)/shard_map/all_gather | solution.py:9
  789.8 2.6 maximum_multiply_fusion
  792.4 5.4 copy.16
  799.0 2.9 fusion.4
  801.9 290.3 %reduce-scatter.4.cloned.1.call-done = f32[32,1024]{1,0:T(8,128)} async-done(((f32[1024,1024]{1,0:T(8,128)}), f32[32,1024]{1,0:T(8,128)}) %reduce-scatter.4.cloned.1.call-update) | async-done | bytes 131088
  1094.1 3.3 fusion.5
  1097.4 64.5 %all-reduce.150.cloned.1.call-done = f32[32,1024]{0,1:T(8,128)} async-done(((f32[32,1024]{0,1:T(8,128)}), f32[32,1024]{0,1:T(8,128)}) %all-reduce.150.cloned.1.call-update) | async-done | bytes 131088 | tf_op jit(solution)/shard_map/psum | solution.py:135
  (908 shorter events, 477.5 us)
Async XLA Ops:
  7.2 272.5 %copy-start = (bf16[1024,512]{1,0:T(8,128)(2,1)S(1)}, bf16[1024,512]{1,0:T(8,128)(2,1)}, u32[]{:S(2)}) copy-start(bf16[1024,512]{1,0:T(8,128)(2,1)} %param.16) | copy-start | bytes 3145732
  7.2 1085.0 %reduce-scatter.4.cloned.1.call-start = ((), (), s32[]{:S(2)}) async-start(), calls=%async_computation.2 | async-start | bytes 4325376
  65.9 103.9 %copy-start.35 = (f32[1,128,256]{2,1,0:T(8,128)}, f32[1,128,256]{2,1,0:T(8,128)S(1)}, u32[]{:S(2)}) copy-start(f32[1,128,256]{2,1,0:T(8,128)S(1)} %get-tuple-element.512) | copy-start | bytes 393220
  290.7 125.0 %copy-start.19 = (f32[1,256,256]{2,1,0:T(8,128)}, f32[1,256,256]{2,1,0:T(8,128)S(1)}, u32[]{:S(2)}) copy-start(f32[1,256,256]{2,1,0:T(8,128)S(1)} %get-tuple-element.471) | copy-start | bytes 786436
  303.9 104.0 %copy-start.36 = (f32[1,128,256]{2,1,0:T(8,128)}, f32[1,128,256]{2,1,0:T(8,128)S(1)}, u32[]{:S(2)}) copy-start(f32[1,128,256]{2,1,0:T(8,128)S(1)} %get-tuple-element.520) | copy-start | bytes 393220
  423.9 197.4 %copy-start.12 = (f32[1,512,256]{2,1,0:T(8,128)S(1)}, f32[1,512,256]{2,1,0:T(8,128)}, u32[]{:S(2)}) copy-start(f32[1,512,256]{2,1,0:T(8,128)} %add.1249) | copy-start | bytes 1572868
  425.4 193.3 %copy-start.13 = (f32[1,512,256]{2,1,0:T(8,128)S(1)}, f32[1,512,256]{2,1,0:T(8,128)}, u32[]{:S(2)}) copy-start(f32[1,512,256]{2,1,0:T(8,128)} %add.1274) | copy-start | bytes 1572868
  426.8 197.2 %copy-start.14 = (f32[1,512,256]{2,1,0:T(8,128)S(1)}, f32[1,512,256]{2,1,0:T(8,128)}, u32[]{:S(2)}) copy-start(f32[1,512,256]{2,1,0:T(8,128)} %add.1276) | copy-start | bytes 1572868
  442.9 183.6 %copy-start.128 = (f32[1,1,256]{2,1,0:T(1,128)S(1)}, f32[1,1,256]{2,1,0:T(1,128)}, u32[]{:S(2)}) copy-start(f32[1,1,256]{2,1,0:T(1,128)} %get-tuple-element.607) | copy-start | bytes 3076
  442.9 183.6 %copy-start.129 = (f32[1,1,256]{2,1,0:T(1,128)S(1)}, f32[1,1,256]{2,1,0:T(1,128)}, u32[]{:S(2)}) copy-start(f32[1,1,256]{2,1,0:T(1,128)} %get-tuple-element.608) | copy-start | bytes 3076
  442.9 183.6 %copy-start.130 = (f32[1,1,256]{2,1,0:T(1,128)S(1)}, f32[1,1,256]{2,1,0:T(1,128)}, u32[]{:S(2)}) copy-start(f32[1,1,256]{2,1,0:T(1,128)} %get-tuple-element.627) | copy-start | bytes 3076
  442.9 183.6 %copy-start.131 = (f32[1,1,256]{2,1,0:T(1,128)S(1)}, f32[1,1,256]{2,1,0:T(1,128)}, u32[]{:S(2)}) copy-start(f32[1,1,256]{2,1,0:T(1,128)} %get-tuple-element.638) | copy-start | bytes 3076
  443.0 183.7 %copy-start.90 = (f32[1,2,256]{2,1,0:T(2,128)S(1)}, f32[1,2,256]{2,1,0:T(2,128)}, u32[]{:S(2)}) copy-start(f32[1,2,256]{2,1,0:T(2,128)} %get-tuple-element.648) | copy-start | bytes 6148
  443.0 183.7 %copy-start.89 = (f32[1,2,256]{2,1,0:T(2,128)S(1)}, f32[1,2,256]{2,1,0:T(2,128)}, u32[]{:S(2)}) copy-start(f32[1,2,256]{2,1,0:T(2,128)} %get-tuple-element.647) | copy-start | bytes 6148
  447.7 179.0 %copy-start.126 = (f32[1,1,256]{2,1,0:T(1,128)S(1)}, f32[1,1,256]{2,1,0:T(1,128)}, u32[]{:S(2)}) copy-start(f32[1,1,256]{2,1,0:T(1,128)} %get-tuple-element.636) | copy-start | bytes 3076
  447.7 179.0 %copy-start.127 = (f32[1,1,256]{2,1,0:T(1,128)S(1)}, f32[1,1,256]{2,1,0:T(1,128)}, u32[]{:S(2)}) copy-start(f32[1,1,256]{2,1,0:T(1,128)} %get-tuple-element.637) | copy-start | bytes 3076
  447.7 179.1 %copy-start.73 = (f32[1,3,256]{2,1,0:T(4,128)S(1)}, f32[1,3,256]{2,1,0:T(4,128)}, u32[]{:S(2)}) copy-start(f32[1,3,256]{2,1,0:T(4,128)} %slice.1200) | copy-start | bytes 9220
  447.7 179.1 %copy-start.74 = (f32[1,3,256]{2,1,0:T(4,128)S(1)}, f32[1,3,256]{2,1,0:T(4,128)}, u32[]{:S(2)}) copy-start(f32[1,3,256]{2,1,0:T(4,128)} %slice.1231) | copy-start | bytes 9220
  447.7 179.1 %copy-start.81 = (f32[1,3,256]{2,1,0:T(4,128)S(1)}, f32[1,3,256]{2,1,0:T(4,128)}, u32[]{:S(2)}) copy-start(f32[1,3,256]{2,1,0:T(4,128)} %slice.1235) | copy-start | bytes 9220
  447.7 179.1 %copy-start.82 = (f32[1,3,256]{2,1,0:T(4,128)S(1)}, f32[1,3,256]{2,1,0:T(4,128)}, u32[]{:S(2)}) copy-start(f32[1,3,256]{2,1,0:T(4,128)} %slice.1239) | copy-start | bytes 9220
  447.7 179.1 %copy-start.122 = (f32[1,1,256]{2,1,0:T(1,128)S(1)}, f32[1,1,256]{2,1,0:T(1,128)}, u32[]{:S(2)}) copy-start(f32[1,1,256]{2,1,0:T(1,128)} %slice.1531) | copy-start | bytes 3076
  447.7 179.2 %copy-start.120 = (f32[1,1,256]{2,1,0:T(1,128)S(1)}, f32[1,1,256]{2,1,0:T(1,128)}, u32[]{:S(2)}) copy-start(f32[1,1,256]{2,1,0:T(1,128)} %slice.1508) | copy-start | bytes 3076
  447.8 179.4 %copy-start.63 = (f32[1,7,256]{2,1,0:T(8,128)S(1)}, f32[1,7,256]{2,1,0:T(8,128)}, u32[]{:S(2)}) copy-start(f32[1,7,256]{2,1,0:T(8,128)} %slice.1190) | copy-start | bytes 21508
  447.8 179.4 %copy-start.64 = (f32[1,7,256]{2,1,0:T(8,128)S(1)}, f32[1,7,256]{2,1,0:T(8,128)}, u32[]{:S(2)}) copy-start(f32[1,7,256]{2,1,0:T(8,128)} %slice.1237) | copy-start | bytes 21508
  447.8 179.4 %copy-start.77 = (f32[1,7,256]{2,1,0:T(8,128)S(1)}, f32[1,7,256]{2,1,0:T(8,128)}, u32[]{:S(2)}) copy-start(f32[1,7,256]{2,1,0:T(8,128)} %slice.1241) | copy-start | bytes 21508
  447.8 179.4 %copy-start.78 = (f32[1,7,256]{2,1,0:T(8,128)S(1)}, f32[1,7,256]{2,1,0:T(8,128)}, u32[]{:S(2)}) copy-start(f32[1,7,256]{2,1,0:T(8,128)} %slice.1245) | copy-start | bytes 21508
  485.0 142.2 %copy-start.119 = (f32[1,1,256]{2,1,0:T(1,128)S(1)}, f32[1,1,256]{2,1,0:T(1,128)}, u32[]{:S(2)}) copy-start(f32[1,1,256]{2,1,0:T(1,128)} %slice.1536) | copy-start | bytes 3076
  548.4 78.9 %copy-start.118 = (f32[1,1,256]{2,1,0:T(1,128)S(1)}, f32[1,1,256]{2,1,0:T(1,128)}, u32[]{:S(2)}) copy-start(f32[1,1,256]{2,1,0:T(1,128)} %slice.1507) | copy-start | bytes 3076
  705.5 77.2 %copy-start.75 = (f32[1,256]{1,0:T(1,128)S(1)}, f32[1,256]{1,0:T(1,128)}, u32[]{:S(2)}) copy-start(f32[1,256]{1,0:T(1,128)} %custom-call) | copy-start | bytes 3076
  705.5 77.2 %copy-start.76 = (f32[1,256]{1,0:T(1,128)S(1)}, f32[1,256]{1,0:T(1,128)}, u32[]{:S(2)}) copy-start(f32[1,256]{1,0:T(1,128)} %custom-call.1) | copy-start | bytes 3076
  797.8 296.3 %copy-start.25 = (bf16[512,256]{1,0:T(8,128)(2,1)S(1)}, bf16[512,256]{1,0:T(8,128)(2,1)}, u32[]{:S(2)}) copy-start(bf16[512,256]{1,0:T(8,128)(2,1)} %copy-done.24) | copy-start | bytes 786436
  797.8 364.1 %all-reduce.150.cloned.1.call-start = ((), (), s32[]{:S(2)}) async-start(), calls=%async_computation.1 | async-start | bytes 1048576 | tf_op jit(solution)/shard_map/psum | solution.py:135
  (104 other events, 1087.9 us)
Sparse Core Ops, SparseCore 0:
  797.9 294.2 reduce-scatter.3
  1094.5 67.3 all-reduce.149
where the time goes:
time: 1190 us; the launch traced here: 1170 us
  local copies, waits for them, and re-layouts  405 us (34%)
  waiting for transfers between devices  355 us (30%)
  blocking collectives  258 us (22%)
  other arithmetic  124 us (10%)
  between operations  17 us (1%)
    unnamed x3, waiting for transfers between devices  290 us
    all_gather x8, blocking collectives, prefix(): everything = jax.tree.map(lambda part: lax.all_gather(part, axis), x)  258 us
    slice x132, local copies, waits for them, and re-layouts, on_device(): lax.associative_scan(complex_combine, (next_re, next_im, adjoint_drive[.....  185 us
    slice x120, local copies, waits for them, and re-layouts, on_device(): lax.associative_scan(complex_combine, (lam_re, lam_im, drive_term[..., :s...  148 us
    psum x1, waiting for transfers between devices, on_device(): my_rows = lax.psum(shares, 'dp')  64.5 us
    select_n x64, other arithmetic, lap(): return jax.tree.map(lambda a, b: jnp.where(reached, a, b), new, before)  38.3 us
  transfers between devices with their start and end apart: 2, of which 2 were waited for; matrix products, arithmetic and copies ran while one was open for 1% of the time, Pallas kernels for 0%

commit v1 on v0

v1 whole, which is shorter than its diff:
```python
import jax
import jax.numpy as jnp
from jax import lax
from jax.experimental import pallas as pl
from jax.experimental.pallas import tpu as pltpu
from jax.sharding import PartitionSpec as P

MESH = pl.DeviceIdType.MESH
F32, BF16 = jnp.float32, jnp.bfloat16
ROWS, WIDTH, STATES = 512, 1024, 256
SUB = 8
LAPS = ROWS // SUB
NX, NY, NZ = 4, 4, 8
PEERS = NY * NZ
DP = 2 * NX
SCALE = float(8 * 16384) ** -0.5


def turn(time, decay, frequency):
    damping = jnp.exp(-(time * decay))
    phase = time * frequency
    n = jnp.floor(phase * 0.6366197723675814 + 0.5)
    r = ((phase - n * 1.5703125) - n * 4.837512969970703125e-4) - n * 7.54978995489188216e-8
    q = n.astype(jnp.int32)
    z = r * r
    sine = r + r * z * (-1.6666654611e-1 + z * (8.3321608736e-3 + z * -1.9515295891e-4))
    cosine = (1.0 - 0.5 * z) + z * z * (
        4.166664568298827e-2 + z * (-1.388731625493765e-3 + z * 2.443315711809948e-5)
    )
    swap = (q & 1) == 1
    a = jnp.where(swap, sine, cosine)
    b = jnp.where(swap, cosine, sine)
    re = jnp.where(((q + 1) & 2) == 2, -a, a)
    im = jnp.where((q & 2) == 2, -b, b)
    return damping * re, damping * im


def cmul(ar, ai, br, bi):
    return ar * br - ai * bi, ar * bi + ai * br


def cmulc(ar, ai, br, bi):
    return ar * br + ai * bi, ar * bi - ai * br


def kernel(
    x_hbm, step_ref, decay_ref, freq_ref, win_hbm, wout_hbm, skip_ref, cot_hbm,
    out_hbm, ig_hbm, gin_ref, gout_ref,
    xc, wio, xct, stb, lam, drv, pairs, outs, chunk, msg, rmsg, own, theirs, partner,
    r1, r2, r3, fin,
    load_sem, store_sem, pre_sem, pair_sem, ring_sem, z_sem, fin_sem,
):
    dp = lax.axis_index("dp")
    ctx = lax.axis_index("context")
    core, x = lax.rem(dp, 2), lax.div(dp, 2)
    y, z = lax.rem(ctx, NY), lax.div(ctx, NY)
    other = 1 - core

    barrier = pltpu.get_barrier_semaphore()

    def greet_context(d, _):
        pl.semaphore_signal(barrier, inc=1, device_id=(dp, lax.rem(ctx + d, PEERS)), device_id_type=MESH)
        return 0

    def greet_dp(d, _):
        pl.semaphore_signal(barrier, inc=1, device_id=(lax.rem(dp + d, DP), ctx), device_id_type=MESH)
        return 0

    loads = [
        pltpu.make_async_copy(x_hbm, xc.at[0], load_sem.at[0]),
        pltpu.make_async_copy(win_hbm, wio.at[0], load_sem.at[1]),
        pltpu.make_async_copy(cot_hbm, xc.at[1], load_sem.at[2]),
        pltpu.make_async_copy(wout_hbm, wio.at[1], load_sem.at[3]),
    ]
    for load in loads:
        load.start()
    lax.fori_loop(1, PEERS, greet_context, 0)
    lax.fori_loop(1, DP, greet_dp, 0)

    decay = [decay_ref[:, g * 128 : (g + 1) * 128] for g in range(2)]
    freq = [freq_ref[:, g * 128 : (g + 1) * 128] for g in range(2)]
    gain = []
    for g in range(2):
        v = 2.0 * decay[g]
        s = jnp.ones_like(v)
        for k in range(9, 1, -1):
            s = 1.0 - v * (1.0 / k) * s
        gain.append(jnp.sqrt(v * s))

    for r in range(ROWS // 128):
        line = jnp.broadcast_to(step_ref[:, r * 128 : (r + 1) * 128], (128, 128))
        stb[r * 128 : (r + 1) * 128, :] = line.T

    def lam_block(i, _):
        rows = pl.ds(pl.multiple_of(i * 32, 32), 32)
        st = stb[rows, :]
        for g in range(2):
            re, im = turn(st, decay[g], freq[g])
            lam[g, rows, :] = re
            lam[2 + g, rows, :] = im
        return 0

    lax.fori_loop(0, ROWS // 32, lam_block, 0)

    for m in range(2):
        loads[2 * m].wait()
        loads[2 * m + 1].wait()
        for nb in range(2):
            res = jnp.dot(xc[m], wio[m, :, nb * 256 : (nb + 1) * 256], preferred_element_type=F32)
            for g in range(2):
                part = res[:, g * 128 : (g + 1) * 128]
                drv[m, 2 * nb + g] = part * gain[g] if m == 0 else part

    def scan_step(j, carry, store):
        f, b, total = carry[:4], carry[4:8], carry[8]
        rf = pl.ds(j, SUB, stride=LAPS)
        rb = pl.ds(LAPS - 1 - j, SUB, stride=LAPS)
        nf, nb = [None] * 4, [None] * 4
        for g in range(2):
            re, im = cmul(lam[g, rf, :], lam[2 + g, rf, :], f[g], f[2 + g])
            nf[g] = re + drv[0, g, rf, :]
            nf[2 + g] = im + drv[0, 2 + g, rf, :]
            ar = drv[1, g, rb, :] + b[g]
            ai = drv[1, 2 + g, rb, :] + b[2 + g]
            if store:
                drv[0, g, rf, :] = nf[g]
                drv[0, 2 + g, rf, :] = nf[2 + g]
                drv[1, g, rb, :] = ar
                drv[1, 2 + g, rb, :] = ai
            nb[g], nb[2 + g] = cmulc(lam[g, rb, :], lam[2 + g, rb, :], ar, ai)
        if not store:
            total = total + stb[rf, :]
        return (*nf, *nb, total)

    zero = jnp.zeros((SUB, 128), F32)
    summary = lax.fori_loop(0, LAPS, lambda j, c: scan_step(j, c, False), (zero,) * 9)
    for k in range(8):
        chunk[4 + k] = summary[k]
    for g in range(2):
        chunk[g], chunk[2 + g] = turn(jnp.minimum(summary[8], 8.0e6), decay[g], freq[g])
    msg[...] = jnp.zeros_like(msg)

    def pass_chunks(entering, keep):
        f, b = list(entering[:4]), list(entering[4:])
        for s in range(SUB):
            e = SUB - 1 - s
            for g in range(2):
                if keep:
                    for h in (g, 2 + g):
                        chunk[12 + h, s : s + 1, :] = f[h]
                        chunk[16 + h, e : e + 1, :] = b[h]
                re, im = cmul(chunk[g, s : s + 1, :], chunk[2 + g, s : s + 1, :], f[g], f[2 + g])
                f[g] = re + chunk[4 + g, s : s + 1, :]
                f[2 + g] = im + chunk[6 + g, s : s + 1, :]
                re, im = cmulc(chunk[g, e : e + 1, :], chunk[2 + g, e : e + 1, :], b[g], b[2 + g])
                b[g] = re + chunk[8 + g, e : e + 1, :]
                b[2 + g] = im + chunk[10 + g, e : e + 1, :]
        return f + b

    leave = pass_chunks((jnp.zeros((1, 128), F32),) * 8, False)
    total = jnp.sum(summary[8], axis=0, keepdims=True)
    for k in range(4):
        msg[0, k : k + 1, :] = leave[k]
        msg[1, k : k + 1, :] = leave[4 + k]
    msg[0, 4:5, :] = total
    msg[1, 4:5, :] = total
    rmsg[ctx] = jnp.zeros((8, 128), F32)

    pl.semaphore_wait(barrier, PEERS - 1 + DP - 1)

    for dz in (4, 3, 5, 2, 6, 1, 7, 0):
        for dy in (2, 1, 3, 0):
            if dz or dy:
                peer = lax.rem(z + dz, NZ) * NY + lax.rem(y + dy, NY)
                pltpu.make_async_remote_copy(
                    src_ref=msg.at[(peer < ctx).astype(jnp.int32)], dst_ref=rmsg.at[ctx],
                    send_sem=pre_sem.at[0], recv_sem=pre_sem.at[1],
                    device_id=(dp, peer), device_id_type=MESH,
                ).start()

    for m in range(2):
        def turn_block(i, _, m=m):
            cols = pl.ds(pl.multiple_of(i * 128, 128), 128)
            xct[m, cols, :] = xc[m, :, cols].T
            return 0

        lax.fori_loop(0, WIDTH // 128, turn_block, 0)

    everyone = pltpu.make_async_remote_copy(
        src_ref=rmsg.at[pl.ds(0, PEERS - 1)], dst_ref=rmsg.at[pl.ds(0, PEERS - 1)],
        send_sem=pre_sem.at[0], recv_sem=pre_sem.at[1],
        device_id=(dp, lax.rem(ctx + 1, PEERS)), device_id_type=MESH,
    )
    everyone.wait_recv()
    everyone.wait_send()

    place = lax.broadcasted_iota(jnp.int32, (PEERS, 128), 0)
    gap = jnp.zeros((PEERS, 128), F32)
    for i in range(PEERS):
        side = 2 * (i < ctx).astype(jnp.int32) - 1
        gap = gap + jnp.where((i - place) * side > 0, rmsg[i, 4:5, :], 0.0)
    gap = jnp.minimum(gap, 8.0e6)
    sign = jnp.where(place < ctx, 1.0, -1.0)
    entering = [None] * 8
    for g in range(2):
        wr, wi = turn(gap, decay[g], sign * freq[g])
        re, im = cmul(wr, wi, rmsg[:, g, :], rmsg[:, 2 + g, :])
        for h, v in ((g, re), (2 + g, im)):
            entering[h] = jnp.sum(jnp.where(place < ctx, v, 0.0), axis=0, keepdims=True)
            entering[4 + h] = jnp.sum(jnp.where(place > ctx, v, 0.0), axis=0, keepdims=True)
    pass_chunks(entering, True)
    start = tuple(chunk[12 + k] for k in range(8)) + (zero,)
    lax.fori_loop(0, LAPS, lambda j, c: scan_step(j, c, True), start)

    def round_block(i, _):
        rows = pl.ds(pl.multiple_of(i * 32, 32), 32)
        for k in range(4):
            pairs[0, rows, k * 128 : (k + 1) * 128] = (drv[1, k, rows, :] * gain[k % 2]).astype(BF16)
            pairs[1, rows, k * 128 : (k + 1) * 128] = drv[0, k, rows, :].astype(BF16)
        return 0

    lax.fori_loop(0, ROWS // 32, round_block, 0)

    def gradient(m, into):
        def rows_block(i, _):
            rows = pl.ds(pl.multiple_of(i * 256, 256), 256)
            res = jnp.dot(xct[m, rows, :], pairs[m], preferred_element_type=F32)
            for zi in range(2):
                for yy in range(NY):
                    top = (zi * NY + yy) * 32
                    for q in range(NX):
                        a = q + m * (yy - q)
                        b = yy + m * (q - yy)
                        into[a, b, 2 * i + zi] = res[top : top + 32, q * 128 : (q + 1) * 128]
            return 0

        lax.fori_loop(0, WIDTH // 256, rows_block, 0)

    spot = x + core * (y - x)
    spot_other = y + core * (x - y)
    gradient(other, theirs)
    swaps = []
    for k, d in enumerate((2, 1, 3, 0)):
        a = lax.rem(spot_other + d, 4)
        swap = pltpu.make_async_remote_copy(
            src_ref=theirs.at[a], dst_ref=partner.at[k],
            send_sem=pair_sem.at[0, k], recv_sem=pair_sem.at[1, k],
            device_id=(2 * x + other, ctx), device_id_type=MESH,
        )
        swap.start()
        swaps.append(swap)
    gradient(core, own)

    def first_ring(d):
        return (2 * lax.rem(x + other * d, 4) + core, z * NY + lax.rem(y + core * d, 4))

    def second_ring(d):
        return (2 * lax.rem(x + core * d, 4) + core, z * NY + lax.rem(y + other * d, 4))

    def send(src, dst, ring, i, device):
        copy = pltpu.make_async_remote_copy(
            src_ref=src, dst_ref=dst, send_sem=ring_sem.at[ring, 0, i], recv_sem=ring_sem.at[ring, 1, i],
            device_id=device, device_id_type=MESH,
        )
        copy.start()
        return copy

    def take_partner(k, d):
        a = lax.rem(spot + d, 4)
        swaps[k].wait_recv()

        def add(i, _):
            own[a, lax.div(i, 2), pl.ds(lax.rem(i, 2) * 4, 4)] += partner[k, lax.div(i, 2), pl.ds(lax.rem(i, 2) * 4, 4)]
            return 0

        lax.fori_loop(0, 8, add, 0)

    def half1(d, h):
        return own.at[lax.rem(spot + d, 4), pl.ds(2 * h, 2)]

    def half2(d, h):
        return own.at[spot, lax.rem(spot_other + d, 4), pl.ds(4 * h, 4)]

    def add_into(view, buf, blocks):
        def add(i, _):
            if len(view.shape) == 4:
                view[lax.div(i, 8), lax.rem(i, 8)] += buf[lax.div(i, 8), lax.rem(i, 8)]
            else:
                view[i] += buf[i]
            return 0

        lax.fori_loop(0, blocks, add, 0)

    copies = [None] * 6
    take_partner(0, 2)
    copies[0] = send(half1(2, 0), r1.at[0], 0, 0, first_ring(1))
    copies[1] = send(half1(2, 1), r1.at[1], 0, 1, first_ring(3))
    take_partner(1, 1)
    copies[2] = send(half1(1, 1), r1.at[2], 0, 2, first_ring(1))
    take_partner(2, 3)
    copies[3] = send(half1(3, 0), r1.at[3], 0, 3, first_ring(3))
    take_partner(3, 0)

    stores = []
    for m in range(2):
        def out_block(i, _, m=m):
            cols = pl.ds(pl.multiple_of(i * 256, 256), 256)
            mixed = lax.dot_general(
                pairs[1 - m], wio[1 - m, cols, :], (((1,), (1,)), ((), ())), preferred_element_type=F32
            )
            outs[m, :, cols] = (mixed + skip_ref[:, cols] * xc[m, :, cols].astype(F32)).astype(BF16)
            return 0

        lax.fori_loop(0, WIDTH // 256, out_block, 0)
        store = pltpu.make_async_copy(outs.at[m], (out_hbm, ig_hbm)[m], store_sem.at[m])
        store.start()
        stores.append(store)

    copies[0].wait_recv()
    add_into(half1(1, 0), r1.at[0], 16)
    copies[4] = send(half1(1, 0), r1.at[4], 0, 4, first_ring(1))
    copies[1].wait_recv()
    add_into(half1(3, 1), r1.at[1], 16)
    copies[5] = send(half1(3, 1), r1.at[5], 0, 5, first_ring(3))
    copies[3].wait_recv()
    add_into(half1(0, 0), r1.at[3], 16)
    copies[2].wait_recv()
    add_into(half1(0, 1), r1.at[2], 16)
    copies[4].wait_recv()
    add_into(half1(0, 0), r1.at[4], 16)
    copies[5].wait_recv()
    add_into(half1(0, 1), r1.at[5], 16)

    more = [None] * 6
    more[0] = send(half2(2, 0), r2.at[0], 1, 0, second_ring(1))
    more[1] = send(half2(2, 1), r2.at[1], 1, 1, second_ring(3))
    more[2] = send(half2(1, 1), r2.at[2], 1, 2, second_ring(1))
    more[3] = send(half2(3, 0), r2.at[3], 1, 3, second_ring(3))
    more[0].wait_recv()
    add_into(half2(1, 0), r2.at[0], 4)
    more[4] = send(half2(1, 0), r2.at[4], 1, 4, second_ring(1))
    more[1].wait_recv()
    add_into(half2(3, 1), r2.at[1], 4)
    more[5] = send(half2(3, 1), r2.at[5], 1, 5, second_ring(3))
    more[3].wait_recv()
    add_into(half2(0, 0), r2.at[3], 4)
    more[2].wait_recv()
    add_into(half2(0, 1), r2.at[2], 4)
    more[4].wait_recv()
    add_into(half2(0, 0), r2.at[4], 4)
    more[5].wait_recv()
    add_into(half2(0, 1), r2.at[5], 4)

    for dz in (4, 3, 5, 2, 6, 1, 7):
        zz = lax.rem(z + dz, NZ)
        pltpu.make_async_remote_copy(
            src_ref=own.at[spot, spot_other, zz], dst_ref=r3.at[z],
            send_sem=z_sem.at[0], recv_sem=z_sem.at[1],
            device_id=(dp, zz * NY + y), device_id_type=MESH,
        ).start()
    r3[z] = own[spot, spot_other, z]
    column = pltpu.make_async_remote_copy(
        src_ref=r3.at[pl.ds(0, NZ - 1)], dst_ref=r3.at[pl.ds(0, NZ - 1)],
        send_sem=z_sem.at[0], recv_sem=z_sem.at[1],
        device_id=(dp, lax.rem(z + 1, NZ) * NY + y), device_id_type=MESH,
    )
    column.wait_recv()
    column.wait_send()
    piece = r3[0]
    for k in range(1, NZ):
        piece = piece + r3[k]
    mine = core * NX + x
    fin[mine] = piece * SCALE
    for d in (4, 5, 3, 2, 6, 7, 1):
        peer = lax.rem(dp + d, DP)
        pltpu.make_async_remote_copy(
            src_ref=fin.at[mine], dst_ref=fin.at[mine],
            send_sem=fin_sem.at[0], recv_sem=fin_sem.at[1],
            device_id=(peer, ctx), device_id_type=MESH,
        ).start()
    row = pltpu.make_async_remote_copy(
        src_ref=fin.at[pl.ds(0, DP - 1)], dst_ref=fin.at[pl.ds(0, DP - 1)],
        send_sem=fin_sem.at[0], recv_sem=fin_sem.at[1],
        device_id=(lax.rem(dp + 1, DP), ctx), device_id_type=MESH,
    )
    row.wait_recv()
    row.wait_send()
    for q in range(NX):
        gin_ref[:, q * 128 : (q + 1) * 128] = fin[q]
        gout_ref[:, q * 128 : (q + 1) * 128] = fin[NX + q]

    for copy in swaps + copies + more:
        copy.wait_send()
    for store in stores:
        store.wait()


def on_device(inputs, step_size, decay_rate, frequency, input_proj, output_proj, skip_gain, cotangent):
    vmem = pl.BlockSpec(memory_space=pltpu.VMEM)
    hbm = pl.BlockSpec(memory_space=pl.ANY)
    out, ig, gin, gout = pl.pallas_call(
        kernel,
        out_shape=(
            jax.ShapeDtypeStruct((ROWS, WIDTH), BF16),
            jax.ShapeDtypeStruct((ROWS, WIDTH), BF16),
            jax.ShapeDtypeStruct((WIDTH // PEERS, 2 * STATES), F32),
            jax.ShapeDtypeStruct((WIDTH // PEERS, 2 * STATES), F32),
        ),
        in_specs=[hbm, vmem, vmem, vmem, hbm, hbm, vmem, hbm],
        out_specs=(hbm, hbm, vmem, vmem),
        scratch_shapes=[
            pltpu.VMEM((2, ROWS, WIDTH), BF16),
            pltpu.VMEM((2, WIDTH, 2 * STATES), BF16),
            pltpu.VMEM((2, WIDTH, ROWS), BF16),
            pltpu.VMEM((ROWS, 128), F32),
            pltpu.VMEM((4, ROWS, 128), F32),
            pltpu.VMEM((2, 4, ROWS, 128), F32),
            pltpu.VMEM((2, ROWS, 2 * STATES), BF16),
            pltpu.VMEM((2, ROWS, WIDTH), BF16),
            pltpu.VMEM((20, SUB, 128), F32),
            pltpu.VMEM((2, 8, 128), F32),
            pltpu.VMEM((PEERS, 8, 128), F32),
            pltpu.VMEM((4, 4, NZ, 32, 128), F32),
            pltpu.VMEM((4, 4, NZ, 32, 128), F32),
            pltpu.VMEM((4, 4, NZ, 32, 128), F32),
            pltpu.VMEM((6, 2, NZ, 32, 128), F32),
            pltpu.VMEM((6, 4, 32, 128), F32),
            pltpu.VMEM((NZ, 32, 128), F32),
            pltpu.VMEM((DP, 32, 128), F32),
            pltpu.SemaphoreType.DMA((4,)),
            pltpu.SemaphoreType.DMA((2,)),
            pltpu.SemaphoreType.DMA((2,)),
            pltpu.SemaphoreType.DMA((2, 4)),
            pltpu.SemaphoreType.DMA((2, 2, 6)),
            pltpu.SemaphoreType.DMA((2,)),
            pltpu.SemaphoreType.DMA((2,)),
        ],
        compiler_params=pltpu.CompilerParams(
            collective_id=0, has_side_effects=True, vmem_limit_bytes=56 * 1024 * 1024
        ),
    )(
        inputs.reshape(ROWS, WIDTH), step_size, decay_rate.reshape(1, STATES), frequency.reshape(1, STATES),
        input_proj, output_proj, skip_gain.reshape(1, WIDTH), cotangent.reshape(ROWS, WIDTH),
    )
    return out.reshape(1, ROWS, WIDTH), ig.reshape(1, ROWS, WIDTH), gin, gout


def solution(mesh):
    in_specs = (
        P("dp", "context", None), P("dp", "context"), P(), P(), P(), P(), P(), P("dp", "context", None),
    )
    out_specs = (
        P("dp", "context", None), P("dp", "context", None), P("context", None), P("context", None),
    )
    return jax.shard_map(on_device, mesh=mesh, in_specs=in_specs, out_specs=out_specs, check_vma=False)
```

time: 1190 us -> 64.3 us (0.05); the launches traced: 1170 us -> 64.1 us
  local copies, waits for them, and re-layouts: 405 us -> 4.82 us
  waiting for transfers between devices: 355 us -> 0 us
  blocking collectives: 258 us -> 0 us
  other arithmetic: 124 us -> 0 us
  Pallas kernels: 0 us -> 58.7 us
  between operations: 17 us -> 0.65 us
    slice x256 -> x0, local copies, waits for them, and re-layouts: 335 us -> none  [the longest x132 185 us: on_device(): lax.associative_scan(complex_combine, (next_re, next_im, adjoint_drive[.....]
    unnamed x3 -> x0, waiting for transfers between devices: 290 us -> none
    all_gather x8 -> x0, blocking collectives: 258 us -> none  [prefix(): everything = jax.tree.map(lambda part: lax.all_gather(part, axis), x)]
    psum x1 -> x0, waiting for transfers between devices: 64.5 us -> none  [on_device(): my_rows = lax.psum(shares, 'dp')]
    pallas_call x0 -> x1, Pallas kernels: none -> 58.7 us  [on_device(): pl.pallas_call(kernel, out_shape=(jax.ShapeDtypeStruct((ROWS, WIDTH), BF1...]
    add x115 -> x0, other arithmetic: 56.3 us -> none  [the longest x28 23.6 us: complex_combine(): later_are * early_bim + later_aim * early_bre + later_bim]
    pad x128 -> x0, local copies, waits for them, and re-layouts: 38.7 us -> none  [the longest x64 23.1 us: on_device(): lax.associative_scan(complex_combine, (next_re, next_im, adjoint_drive[.....]
    select_n x64 -> x0, other arithmetic: 38.3 us -> none  [lap(): return jax.tree.map(lambda a, b: jnp.where(reached, a, b), new, before)]
  transfers between devices with their start and end apart: 2 -> 0, of which waited for: 2 -> 0; matrix products, arithmetic and copies ran while one was open for 1% -> 0% of each run, Pallas kernels for 0% -> 0%
where the time goes in v1:
time: 64.3 us; the launch traced here: 64.1 us
  Pallas kernels  58.7 us (91%)
  local copies, waits for them, and re-layouts  4.82 us (7%)
  between operations  0.65 us (1%)
    pallas_call x1, Pallas kernels, on_device(): pl.pallas_call(kernel, out_shape=(jax.ShapeDtypeStruct((ROWS, WIDTH), BF1...  58.7 us
    unnamed x10, local copies, waits for them, and re-layouts  4.82 us

profile of v1, /device:TPU:1, one launch (start us, length us, event | category | flops | bytes accessed | tf_op | source)
XLA Modules:
  0.0 64.1 jit_solution(1417371095819848377)
XLA Ops:
  0.6 58.7 %shard_map.111 = (bf16[512,1024]{1,0:T(8,128)(2,1)}, bf16[512,1024]{1,0:T(8,128)(2,1)}, f32[32,512]{1,0:T(8,128)}, f32[32,512]{1,0:T(8,128)}) custom-call(bf16[512,1024]{1,0:T(8,128)(2,1)} %bitcast.9, f32[1,512]{1,0:T(1,128)} %step_ref.1, f32[1,256]{1,0:T(1,128)} %bitcast.12, f32[1,256]{1,0:T(1,128)} %bitcast.13, bf16[1024,512]{1,0:T(8,128)(2,1)} %win_hbm.1, ...), custom_call_target="tpu_custom_call" | custom-call | tf_op jit(solution)/shard_map/pallas_call | solution.py:401
  59.3 0.0 copy-start
  59.3 2.4 %copy.16 = bf16[1,512,1024]{2,1,0:T(8,128)(2,1)} copy(bf16[1,512,1024]{2,1,0:T(8,128)(2,1)} %bitcast.8) | data formatting | bytes 2097152
  61.7 0.0 copy-done
  61.7 0.0 copy-start.2
  61.7 1.0 %copy.17 = bf16[1,512,1024]{2,1,0:T(8,128)(2,1)} copy(bf16[1,512,1024]{2,1,0:T(8,128)(2,1)S(1)} %bitcast.7) | data formatting | bytes 2097152
  62.6 0.0 copy-done.2
  62.6 0.0 copy-start.1
  62.6 0.6 copy.18
  63.3 0.2 copy-done.1
  63.5 0.6 copy.19
Async XLA Ops:
  59.3 2.4 %copy-start = (bf16[512,1024]{1,0:T(8,128)(2,1)S(1)}, bf16[512,1024]{1,0:T(8,128)(2,1)}, u32[]{:S(2)}) copy-start(bf16[512,1024]{1,0:T(8,128)(2,1)} %get-tuple-element.9) | copy-start | bytes 3145732
  61.7 1.0 %copy-start.2 = (f32[32,512]{1,0:T(8,128)S(1)}, f32[32,512]{1,0:T(8,128)}, u32[]{:S(2)}) copy-start(f32[32,512]{1,0:T(8,128)} %get-tuple-element.18) | copy-start | bytes 196612
  62.6 0.9 %copy-start.1 = (f32[32,512]{1,0:T(8,128)S(1)}, f32[32,512]{1,0:T(8,128)}, u32[]{:S(2)}) copy-start(f32[32,512]{1,0:T(8,128)} %get-tuple-element.19) | copy-start | bytes 196612

commit v2 on v1

--- a/solution.py
+++ b/solution.py
@@ -10,6 +10,7 @@
 ROWS, WIDTH, STATES = 512, 1024, 256
 SUB = 8
 LAPS = ROWS // SUB
+PITCH = LAPS + 1
 NX, NY, NZ = 4, 4, 8
 PEERS = NY * NZ
 DP = 2 * NX
@@ -89,10 +90,12 @@
 
     for r in range(ROWS // 128):
         line = jnp.broadcast_to(step_ref[:, r * 128 : (r + 1) * 128], (128, 128))
-        stb[r * 128 : (r + 1) * 128, :] = line.T
+        turned = line.T
+        for s in (0, 1):
+            stb[pl.ds((2 * r + s) * PITCH, LAPS), :] = turned[s * LAPS : (s + 1) * LAPS]
 
     def lam_block(i, _):
-        rows = pl.ds(pl.multiple_of(i * 32, 32), 32)
+        rows = pl.ds(lax.div(i, 2) * PITCH + lax.rem(i, 2) * 32, 32)
         st = stb[rows, :]
         for g in range(2):
             re, im = turn(st, decay[g], freq[g])
@@ -109,12 +112,14 @@
             res = jnp.dot(xc[m], wio[m, :, nb * 256 : (nb + 1) * 256], preferred_element_type=F32)
             for g in range(2):
                 part = res[:, g * 128 : (g + 1) * 128]
-                drv[m, 2 * nb + g] = part * gain[g] if m == 0 else part
+                part = part * gain[g] if m == 0 else part
+                for s in range(SUB):
+                    drv[m, 2 * nb + g, s * PITCH : s * PITCH + LAPS, :] = part[s * LAPS : (s + 1) * LAPS]
 
     def scan_step(j, carry, store):
         f, b, total = carry[:4], carry[4:8], carry[8]
-        rf = pl.ds(j, SUB, stride=LAPS)
-        rb = pl.ds(LAPS - 1 - j, SUB, stride=LAPS)
+        rf = pl.ds(j, SUB, stride=PITCH)
+        rb = pl.ds(LAPS - 1 - j, SUB, stride=PITCH)
         nf, nb = [None] * 4, [None] * 4
         for g in range(2):
             re, im = cmul(lam[g, rf, :], lam[2 + g, rf, :], f[g], f[2 + g])
@@ -214,9 +219,10 @@
 
     def round_block(i, _):
         rows = pl.ds(pl.multiple_of(i * 32, 32), 32)
+        held = pl.ds(lax.div(i, 2) * PITCH + lax.rem(i, 2) * 32, 32)
         for k in range(4):
-            pairs[0, rows, k * 128 : (k + 1) * 128] = (drv[1, k, rows, :] * gain[k % 2]).astype(BF16)
-            pairs[1, rows, k * 128 : (k + 1) * 128] = drv[0, k, rows, :].astype(BF16)
+            pairs[0, rows, k * 128 : (k + 1) * 128] = (drv[1, k, held, :] * gain[k % 2]).astype(BF16)
+            pairs[1, rows, k * 128 : (k + 1) * 128] = drv[0, k, held, :].astype(BF16)
         return 0
 
     lax.fori_loop(0, ROWS // 32, round_block, 0)
@@ -412,9 +418,9 @@
             pltpu.VMEM((2, ROWS, WIDTH), BF16),
             pltpu.VMEM((2, WIDTH, 2 * STATES), BF16),
             pltpu.VMEM((2, WIDTH, ROWS), BF16),
-            pltpu.VMEM((ROWS, 128), F32),
-            pltpu.VMEM((4, ROWS, 128), F32),
-            pltpu.VMEM((2, 4, ROWS, 128), F32),
+            pltpu.VMEM((SUB * PITCH, 128), F32),
+            pltpu.VMEM((4, SUB * PITCH, 128), F32),
+            pltpu.VMEM((2, 4, SUB * PITCH, 128), F32),
             pltpu.VMEM((2, ROWS, 2 * STATES), BF16),
             pltpu.VMEM((2, ROWS, WIDTH), BF16),
             pltpu.VMEM((20, SUB, 128), F32),

time: 64.3 us -> 56.5 us (0.88)
  Pallas kernels: 58.7 us -> 50.9 us
    pallas_call x1, Pallas kernels: 58.7 us -> 50.9 us  [on_device(): pl.pallas_call(kernel, out_shape=(jax.ShapeDtypeStruct((ROWS, WIDTH), BF1...]
where the time goes in v2:
time: 56.5 us; the launch traced here: 56.4 us
  Pallas kernels  50.9 us (90%)
  local copies, waits for them, and re-layouts  4.82 us (9%)
  between operations  0.65 us (1%)
    pallas_call x1, Pallas kernels, on_device(): pl.pallas_call(kernel, out_shape=(jax.ShapeDtypeStruct((ROWS, WIDTH), BF1...  50.9 us
    unnamed x10, local copies, waits for them, and re-layouts  4.82 us

profile of v2, /device:TPU:1, one launch (start us, length us, event | category | flops | bytes accessed | tf_op | source)
XLA Modules:
  0.0 56.4 jit_solution(12433510649040064172)
XLA Ops:
  0.6 50.9 %shard_map.111 = (bf16[512,1024]{1,0:T(8,128)(2,1)}, bf16[512,1024]{1,0:T(8,128)(2,1)}, f32[32,512]{1,0:T(8,128)}, f32[32,512]{1,0:T(8,128)}) custom-call(bf16[512,1024]{1,0:T(8,128)(2,1)} %bitcast.9, f32[1,512]{1,0:T(1,128)} %step_ref.1, f32[1,256]{1,0:T(1,128)} %bitcast.12, f32[1,256]{1,0:T(1,128)} %bitcast.13, bf16[1024,512]{1,0:T(8,128)(2,1)} %win_hbm.1, ...), custom_call_target="tpu_custom_call" | custom-call | tf_op jit(solution)/shard_map/pallas_call | solution.py:407
  51.5 0.0 copy-start
  51.5 2.4 %copy.16 = bf16[1,512,1024]{2,1,0:T(8,128)(2,1)} copy(bf16[1,512,1024]{2,1,0:T(8,128)(2,1)} %bitcast.8) | data formatting | bytes 2097152
  53.9 0.0 copy-done
  53.9 0.0 copy-start.2
  53.9 1.0 %copy.17 = bf16[1,512,1024]{2,1,0:T(8,128)(2,1)} copy(bf16[1,512,1024]{2,1,0:T(8,128)(2,1)S(1)} %bitcast.7) | data formatting | bytes 2097152
  54.9 0.0 copy-done.2
  54.9 0.0 copy-start.1
  54.9 0.6 %copy.18 = f32[32,512]{1,0:T(8,128)} copy(f32[32,512]{1,0:T(8,128)S(1)} %copy-done.2) | data formatting | bytes 131072
  55.5 0.2 copy-done.1
  55.7 0.6 %copy.19 = f32[32,512]{1,0:T(8,128)} copy(f32[32,512]{1,0:T(8,128)S(1)} %copy-done.1) | data formatting | bytes 131072
Async XLA Ops:
  51.5 2.4 %copy-start = (bf16[512,1024]{1,0:T(8,128)(2,1)S(1)}, bf16[512,1024]{1,0:T(8,128)(2,1)}, u32[]{:S(2)}) copy-start(bf16[512,1024]{1,0:T(8,128)(2,1)} %get-tuple-element.9) | copy-start | bytes 3145732
  53.9 1.0 %copy-start.2 = (f32[32,512]{1,0:T(8,128)S(1)}, f32[32,512]{1,0:T(8,128)}, u32[]{:S(2)}) copy-start(f32[32,512]{1,0:T(8,128)} %get-tuple-element.18) | copy-start | bytes 196612
  54.9 0.9 %copy-start.1 = (f32[32,512]{1,0:T(8,128)S(1)}, f32[32,512]{1,0:T(8,128)}, u32[]{:S(2)}) copy-start(f32[32,512]{1,0:T(8,128)} %get-tuple-element.19) | copy-start | bytes 196612

commit v3 on v2

--- a/solution.py
+++ b/solution.py
@@ -14,6 +14,7 @@
 NX, NY, NZ = 4, 4, 8
 PEERS = NY * NZ
 DP = 2 * NX
+PARTS = 4
 SCALE = float(8 * 16384) ** -0.5
 
 
@@ -46,10 +47,10 @@
 
 def kernel(
     x_hbm, step_ref, decay_ref, freq_ref, win_hbm, wout_hbm, skip_ref, cot_hbm,
-    out_hbm, ig_hbm, gin_ref, gout_ref,
-    xc, wio, xct, stb, lam, drv, pairs, outs, chunk, msg, rmsg, own, theirs, partner,
-    r1, r2, r3, fin,
-    load_sem, store_sem, pre_sem, pair_sem, ring_sem, z_sem, fin_sem,
+    out_ref, ig_ref, gin_ref, gout_ref,
+    xc, wio, xct, stb, lam, drv, pairs, chunk, msg, rmsg, own, theirs, partner,
+    r1, r2, up, r3, fin,
+    load_sem, pre_sem, pair_sem, ring_sem, second_sem, z_sem, fin_sem,
 ):
     dp = lax.axis_index("dp")
     ctx = lax.axis_index("context")
@@ -227,7 +228,7 @@
 
     lax.fori_loop(0, ROWS // 32, round_block, 0)
 
-    def gradient(m, into):
+    def gradient(m, into, then=None):
         def rows_block(i, _):
             rows = pl.ds(pl.multiple_of(i * 256, 256), 256)
             res = jnp.dot(xct[m, rows, :], pairs[m], preferred_element_type=F32)
@@ -237,24 +238,24 @@
                     for q in range(NX):
                         a = q + m * (yy - q)
                         b = yy + m * (q - yy)
-                        into[a, b, 2 * i + zi] = res[top : top + 32, q * 128 : (q + 1) * 128]
+                        into[i, a, b, zi] = res[top : top + 32, q * 128 : (q + 1) * 128]
+            if then is not None:
+                then(i)
             return 0
 
-        lax.fori_loop(0, WIDTH // 256, rows_block, 0)
+        lax.fori_loop(0, PARTS, rows_block, 0)
 
     spot = x + core * (y - x)
     spot_other = y + core * (x - y)
-    gradient(other, theirs)
-    swaps = []
-    for k, d in enumerate((2, 1, 3, 0)):
-        a = lax.rem(spot_other + d, 4)
-        swap = pltpu.make_async_remote_copy(
-            src_ref=theirs.at[a], dst_ref=partner.at[k],
-            send_sem=pair_sem.at[0, k], recv_sem=pair_sem.at[1, k],
+
+    def swap(i):
+        return pltpu.make_async_remote_copy(
+            src_ref=theirs.at[i], dst_ref=partner.at[i],
+            send_sem=pair_sem.at[0, i], recv_sem=pair_sem.at[1, i],
             device_id=(2 * x + other, ctx), device_id_type=MESH,
         )
-        swap.start()
-        swaps.append(swap)
+
+    gradient(other, theirs, lambda i: swap(i).start())
     gradient(core, own)
 
     def first_ring(d):
@@ -263,157 +264,169 @@
     def second_ring(d):
         return (2 * lax.rem(x + core * d, 4) + core, z * NY + lax.rem(y + other * d, 4))
 
-    def send(src, dst, ring, i, device):
+    def half(i, d, h):
+        return own.at[i, lax.rem(spot + d, 4), pl.ds(2 * h, 2)]
+
+    def add_into(view, *bufs):
+        total = view[...]
+        for buf in bufs:
+            total = total + buf[...]
+        view[...] = total
+
+    sent = []
+
+    def send_first(i, slot, src, d):
         copy = pltpu.make_async_remote_copy(
-            src_ref=src, dst_ref=dst, send_sem=ring_sem.at[ring, 0, i], recv_sem=ring_sem.at[ring, 1, i],
-            device_id=device, device_id_type=MESH,
+            src_ref=src, dst_ref=r1.at[i, slot], send_sem=ring_sem.at[0, i, slot], recv_sem=ring_sem.at[1, i, slot],
+            device_id=first_ring(d), device_id_type=MESH,
         )
         copy.start()
+        sent.append(copy)
         return copy
 
-    def take_partner(k, d):
-        a = lax.rem(spot + d, 4)
-        swaps[k].wait_recv()
-
-        def add(i, _):
-            own[a, lax.div(i, 2), pl.ds(lax.rem(i, 2) * 4, 4)] += partner[k, lax.div(i, 2), pl.ds(lax.rem(i, 2) * 4, 4)]
+    firsts = [[None] * 6 for _ in range(PARTS)]
+    seconds = [None] * PARTS
+
+    def begin(i):
+        swap(i).wait_recv()
+
+        def add(a, _):
+            own[i, a] += partner[i, a]
             return 0
 
-        lax.fori_loop(0, 8, add, 0)
-
-    def half1(d, h):
-        return own.at[lax.rem(spot + d, 4), pl.ds(2 * h, 2)]
-
-    def half2(d, h):
-        return own.at[spot, lax.rem(spot_other + d, 4), pl.ds(4 * h, 4)]
-
-    def add_into(view, buf, blocks):
-        def add(i, _):
-            if len(view.shape) == 4:
-                view[lax.div(i, 8), lax.rem(i, 8)] += buf[lax.div(i, 8), lax.rem(i, 8)]
-            else:
-                view[i] += buf[i]
-            return 0
-
-        lax.fori_loop(0, blocks, add, 0)
-
-    copies = [None] * 6
-    take_partner(0, 2)
-    copies[0] = send(half1(2, 0), r1.at[0], 0, 0, first_ring(1))
-    copies[1] = send(half1(2, 1), r1.at[1], 0, 1, first_ring(3))
-    take_partner(1, 1)
-    copies[2] = send(half1(1, 1), r1.at[2], 0, 2, first_ring(1))
-    take_partner(2, 3)
-    copies[3] = send(half1(3, 0), r1.at[3], 0, 3, first_ring(3))
-    take_partner(3, 0)
-
-    stores = []
-    for m in range(2):
-        def out_block(i, _, m=m):
-            cols = pl.ds(pl.multiple_of(i * 256, 256), 256)
-            mixed = lax.dot_general(
-                pairs[1 - m], wio[1 - m, cols, :], (((1,), (1,)), ((), ())), preferred_element_type=F32
+        lax.fori_loop(0, 4, add, 0)
+        firsts[i][0] = send_first(i, 0, half(i, 2, 0), 1)
+        firsts[i][1] = send_first(i, 1, half(i, 2, 1), 3)
+        firsts[i][2] = send_first(i, 2, half(i, 1, 1), 1)
+        firsts[i][3] = send_first(i, 3, half(i, 3, 0), 3)
+
+    def relay(i):
+        firsts[i][0].wait_recv()
+        add_into(half(i, 1, 0), r1.at[i, 0])
+        firsts[i][4] = send_first(i, 4, half(i, 1, 0), 1)
+        firsts[i][1].wait_recv()
+        add_into(half(i, 3, 1), r1.at[i, 1])
+        firsts[i][5] = send_first(i, 5, half(i, 3, 1), 3)
+
+    def turn_corner(i):
+        for slot in (2, 3, 4, 5):
+            firsts[i][slot].wait_recv()
+        add_into(half(i, 0, 0), r1.at[i, 3], r1.at[i, 4])
+        add_into(half(i, 0, 1), r1.at[i, 2], r1.at[i, 5])
+        seconds[i] = []
+        for d in (2, 1, 3):
+            copy = pltpu.make_async_remote_copy(
+                src_ref=own.at[i, spot, lax.rem(spot_other + d, 4)], dst_ref=r2.at[i, d - 1],
+                send_sem=second_sem.at[0, i, d - 1], recv_sem=second_sem.at[1, i, d - 1],
+                device_id=second_ring(d), device_id_type=MESH,
             )
-            outs[m, :, cols] = (mixed + skip_ref[:, cols] * xc[m, :, cols].astype(F32)).astype(BF16)
-            return 0
-
-        lax.fori_loop(0, WIDTH // 256, out_block, 0)
-        store = pltpu.make_async_copy(outs.at[m], (out_hbm, ig_hbm)[m], store_sem.at[m])
-        store.start()
-        stores.append(store)
-
-    copies[0].wait_recv()
-    add_into(half1(1, 0), r1.at[0], 16)
-    copies[4] = send(half1(1, 0), r1.at[4], 0, 4, first_ring(1))
-    copies[1].wait_recv()
-    add_into(half1(3, 1), r1.at[1], 16)
-    copies[5] = send(half1(3, 1), r1.at[5], 0, 5, first_ring(3))
-    copies[3].wait_recv()
-    add_into(half1(0, 0), r1.at[3], 16)
-    copies[2].wait_recv()
-    add_into(half1(0, 1), r1.at[2], 16)
-    copies[4].wait_recv()
-    add_into(half1(0, 0), r1.at[4], 16)
-    copies[5].wait_recv()
-    add_into(half1(0, 1), r1.at[5], 16)
-
-    more = [None] * 6
-    more[0] = send(half2(2, 0), r2.at[0], 1, 0, second_ring(1))
-    more[1] = send(half2(2, 1), r2.at[1], 1, 1, second_ring(3))
-    more[2] = send(half2(1, 1), r2.at[2], 1, 2, second_ring(1))
-    more[3] = send(half2(3, 0), r2.at[3], 1, 3, second_ring(3))
-    more[0].wait_recv()
-    add_into(half2(1, 0), r2.at[0], 4)
-    more[4] = send(half2(1, 0), r2.at[4], 1, 4, second_ring(1))
-    more[1].wait_recv()
-    add_into(half2(3, 1), r2.at[1], 4)
-    more[5] = send(half2(3, 1), r2.at[5], 1, 5, second_ring(3))
-    more[3].wait_recv()
-    add_into(half2(0, 0), r2.at[3], 4)
-    more[2].wait_recv()
-    add_into(half2(0, 1), r2.at[2], 4)
-    more[4].wait_recv()
-    add_into(half2(0, 0), r2.at[4], 4)
-    more[5].wait_recv()
-    add_into(half2(0, 1), r2.at[5], 4)
-
-    for dz in (4, 3, 5, 2, 6, 1, 7):
-        zz = lax.rem(z + dz, NZ)
-        pltpu.make_async_remote_copy(
-            src_ref=own.at[spot, spot_other, zz], dst_ref=r3.at[z],
-            send_sem=z_sem.at[0], recv_sem=z_sem.at[1],
-            device_id=(dp, zz * NY + y), device_id_type=MESH,
-        ).start()
-    r3[z] = own[spot, spot_other, z]
+            copy.start()
+            sent.append(copy)
+            seconds[i].append(copy)
+
+    def climb(i):
+        for copy in seconds[i]:
+            copy.wait_recv()
+        up[i] = own[i, spot, spot_other] + r2[i, 0] + r2[i, 1] + r2[i, 2]
+        for k in range(2):
+            goal = 2 * i + k
+
+            @pl.when(z == goal)
+            def _():
+                r3[z] = up[i, k]
+
+            @pl.when(z != goal)
+            def _():
+                pltpu.make_async_remote_copy(
+                    src_ref=up.at[i, k], dst_ref=r3.at[z],
+                    send_sem=z_sem.at[0], recv_sem=z_sem.at[1],
+                    device_id=(dp, goal * NY + y), device_id_type=MESH,
+                ).start()
+
+    def out_block(m, i):
+        cols = slice(i * 256, (i + 1) * 256)
+        mixed = lax.dot_general(
+            pairs[1 - m], wio[1 - m, cols, :], (((1,), (1,)), ((), ())), preferred_element_type=F32
+        )
+        (out_ref, ig_ref)[m][:, cols] = (mixed + skip_ref[:, cols] * xc[m, :, cols].astype(F32)).astype(BF16)
+
+    begin(0)
+    out_block(0, 0)
+    out_block(0, 1)
+    begin(1)
+    out_block(0, 2)
+    out_block(0, 3)
+    begin(2)
+    out_block(1, 0)
+    relay(0)
+    begin(3)
+    out_block(1, 1)
+    relay(1)
+    turn_corner(0)
+    out_block(1, 2)
+    relay(2)
+    turn_corner(1)
+    climb(0)
+    out_block(1, 3)
+    relay(3)
+    turn_corner(2)
+    climb(1)
+    turn_corner(3)
+    climb(2)
+    climb(3)
+
     column = pltpu.make_async_remote_copy(
         src_ref=r3.at[pl.ds(0, NZ - 1)], dst_ref=r3.at[pl.ds(0, NZ - 1)],
         send_sem=z_sem.at[0], recv_sem=z_sem.at[1],
         device_id=(dp, lax.rem(z + 1, NZ) * NY + y), device_id_type=MESH,
     )
     column.wait_recv()
-    column.wait_send()
     piece = r3[0]
     for k in range(1, NZ):
         piece = piece + r3[k]
     mine = core * NX + x
     fin[mine] = piece * SCALE
     for d in (4, 5, 3, 2, 6, 7, 1):
-        peer = lax.rem(dp + d, DP)
         pltpu.make_async_remote_copy(
             src_ref=fin.at[mine], dst_ref=fin.at[mine],
             send_sem=fin_sem.at[0], recv_sem=fin_sem.at[1],
-            device_id=(peer, ctx), device_id_type=MESH,
+            device_id=(lax.rem(dp + d, DP), ctx), device_id_type=MESH,
         ).start()
     row = pltpu.make_async_remote_copy(
         src_ref=fin.at[pl.ds(0, DP - 1)], dst_ref=fin.at[pl.ds(0, DP - 1)],
         send_sem=fin_sem.at[0], recv_sem=fin_sem.at[1],
         device_id=(lax.rem(dp + 1, DP), ctx), device_id_type=MESH,
     )
+    column.wait_send()
+    for i in range(PARTS):
+        swap(i).wait_send()
+    for copy in sent:
+        copy.wait_send()
     row.wait_recv()
-    row.wait_send()
     for q in range(NX):
         gin_ref[:, q * 128 : (q + 1) * 128] = fin[q]
         gout_ref[:, q * 128 : (q + 1) * 128] = fin[NX + q]
-
-    for copy in swaps + copies + more:
-        copy.wait_send()
-    for store in stores:
-        store.wait()
+    row.wait_send()
+
+
+def store_kernel(*refs):
+    sems = refs[8]
+    copies = [pltpu.make_async_copy(refs[k], refs[4 + k], sems.at[k]) for k in range(4)]
+    for copy in copies:
+        copy.start()
+    for copy in copies:
+        copy.wait()
 
 
 def on_device(inputs, step_size, decay_rate, frequency, input_proj, output_proj, skip_gain, cotangent):
     vmem = pl.BlockSpec(memory_space=pltpu.VMEM)
-    hbm = pl.BlockSpec(memory_space=pl.ANY)
-    out, ig, gin, gout = pl.pallas_call(
+    hbm = pl.BlockSpec(memory_space=pltpu.HBM)
+    results = [((ROWS, WIDTH), BF16)] * 2 + [((WIDTH // PEERS, 2 * STATES), F32)] * 2
+    held = pl.pallas_call(
         kernel,
-        out_shape=(
-            jax.ShapeDtypeStruct((ROWS, WIDTH), BF16),
-            jax.ShapeDtypeStruct((ROWS, WIDTH), BF16),
-            jax.ShapeDtypeStruct((WIDTH // PEERS, 2 * STATES), F32),
-            jax.ShapeDtypeStruct((WIDTH // PEERS, 2 * STATES), F32),
-        ),
+        out_shape=tuple(pltpu.VMEM(shape, dtype) for shape, dtype in results),
         in_specs=[hbm, vmem, vmem, vmem, hbm, hbm, vmem, hbm],
-        out_specs=(hbm, hbm, vmem, vmem),
+        out_specs=(vmem,) * 4,
         scratch_shapes=[
             pltpu.VMEM((2, ROWS, WIDTH), BF16),
             pltpu.VMEM((2, WIDTH, 2 * STATES), BF16),
@@ -422,32 +435,39 @@
             pltpu.VMEM((4, SUB * PITCH, 128), F32),
             pltpu.VMEM((2, 4, SUB * PITCH, 128), F32),
             pltpu.VMEM((2, ROWS, 2 * STATES), BF16),
-            pltpu.VMEM((2, ROWS, WIDTH), BF16),
             pltpu.VMEM((20, SUB, 128), F32),
             pltpu.VMEM((2, 8, 128), F32),
             pltpu.VMEM((PEERS, 8, 128), F32),
-            pltpu.VMEM((4, 4, NZ, 32, 128), F32),
-            pltpu.VMEM((4, 4, NZ, 32, 128), F32),
-            pltpu.VMEM((4, 4, NZ, 32, 128), F32),
-            pltpu.VMEM((6, 2, NZ, 32, 128), F32),
-            pltpu.VMEM((6, 4, 32, 128), F32),
+            pltpu.VMEM((PARTS, 4, 4, 2, 32, 128), F32),
+            pltpu.VMEM((PARTS, 4, 4, 2, 32, 128), F32),
+            pltpu.VMEM((PARTS, 4, 4, 2, 32, 128), F32),
+            pltpu.VMEM((PARTS, 6, 2, 2, 32, 128), F32),
+            pltpu.VMEM((PARTS, 3, 2, 32, 128), F32),
+            pltpu.VMEM((PARTS, 2, 32, 128), F32),
             pltpu.VMEM((NZ, 32, 128), F32),
             pltpu.VMEM((DP, 32, 128), F32),
             pltpu.SemaphoreType.DMA((4,)),
             pltpu.SemaphoreType.DMA((2,)),
-            pltpu.SemaphoreType.DMA((2,)),
-            pltpu.SemaphoreType.DMA((2, 4)),
-            pltpu.SemaphoreType.DMA((2, 2, 6)),
+            pltpu.SemaphoreType.DMA((2, PARTS)),
+            pltpu.SemaphoreType.DMA((2, PARTS, 6)),
+            pltpu.SemaphoreType.DMA((2, PARTS, 3)),
             pltpu.SemaphoreType.DMA((2,)),
             pltpu.SemaphoreType.DMA((2,)),
         ],
         compiler_params=pltpu.CompilerParams(
-            collective_id=0, has_side_effects=True, vmem_limit_bytes=56 * 1024 * 1024
+            collective_id=0, has_side_effects=True, vmem_limit_bytes=60 * 1024 * 1024
         ),
     )(
         inputs.reshape(ROWS, WIDTH), step_size, decay_rate.reshape(1, STATES), frequency.reshape(1, STATES),
         input_proj, output_proj, skip_gain.reshape(1, WIDTH), cotangent.reshape(ROWS, WIDTH),
     )
+    out, ig, gin, gout = pl.pallas_call(
+        store_kernel,
+        out_shape=tuple(jax.ShapeDtypeStruct(shape, dtype) for shape, dtype in results),
+        in_specs=[vmem] * 4,
+        out_specs=(hbm,) * 4,
+        scratch_shapes=[pltpu.SemaphoreType.DMA((4,))],
+    )(*(pltpu.with_memory_space_constraint(part, pltpu.VMEM) for part in held))
     return out.reshape(1, ROWS, WIDTH), ig.reshape(1, ROWS, WIDTH), gin, gout
 
 

time: 56.5 us -> 48.6 us (0.86)
  local copies, waits for them, and re-layouts: 4.82 us -> 0 us
  Pallas kernels: 50.9 us -> 47.8 us
    unnamed x10 -> x0, local copies, waits for them, and re-layouts: 4.82 us -> none
    pallas_call x1 -> x2, Pallas kernels: 50.9 us -> 47.8 us  [the longest x1 46.4 us: on_device(): pl.pallas_call(kernel, out_shape=tuple((pltpu.VMEM(shape, dtype) for shap...]
where the time goes in v3:
time: 48.6 us; the launch traced here: 48.4 us
  Pallas kernels  47.8 us (98%)
  between operations  0.64 us (1%)
    pallas_call x1, Pallas kernels, on_device(): pl.pallas_call(kernel, out_shape=tuple((pltpu.VMEM(shape, dtype) for shap...  46.4 us
    pallas_call x1, Pallas kernels, on_device(): pl.pallas_call(store_kernel, out_shape=tuple((jax.ShapeDtypeStruct(shape,...  1.38 us

profile of v3, /device:TPU:1, one launch (start us, length us, event | category | flops | bytes accessed | tf_op | source)
XLA Modules:
  0.0 48.4 jit_solution(17093784987905661212)
XLA Ops:
  0.6 46.4 %shard_map.111 = (bf16[512,1024]{1,0:T(8,128)(2,1)S(1)}, bf16[512,1024]{1,0:T(8,128)(2,1)S(1)}, f32[32,512]{1,0:T(8,128)S(1)}, f32[32,512]{1,0:T(8,128)S(1)}) custom-call(bf16[512,1024]{1,0:T(8,128)(2,1)} %bitcast.7, f32[1,512]{1,0:T(1,128)} %step_ref.1, f32[1,256]{1,0:T(1,128)} %bitcast.10, f32[1,256]{1,0:T(1,128)} %bitcast.11, bf16[1024,512]{1,0:T(8,128)(2,1)} %win_hbm.1, ...), custom_call_target="tpu_custom_call" | custom-call | tf_op jit(solution)/shard_map/pallas_call | solution.py:425
  47.0 1.4 %shard_map.112 = (bf16[512,1024]{1,0:T(8,128)(2,1)}, bf16[512,1024]{1,0:T(8,128)(2,1)}, f32[32,512]{1,0:T(8,128)}, f32[32,512]{1,0:T(8,128)}) custom-call(bf16[512,1024]{1,0:T(8,128)(2,1)S(1)} %get-tuple-element.12.refs_0_, bf16[512,1024]{1,0:T(8,128)(2,1)S(1)} %get-tuple-element.13.refs_1_, f32[32,512]{1,0:T(8,128)S(1)} %get-tuple-element.14.refs_2_, ...), custom_call_target="tpu_custom_call" | custom-call | tf_op jit(solution)/shard_map/pallas_call | solution.py:464

commit v4 on v3

--- a/solution.py
+++ b/solution.py
@@ -46,11 +46,11 @@
 
 
 def kernel(
-    x_hbm, step_ref, decay_ref, freq_ref, win_hbm, wout_hbm, skip_ref, cot_hbm,
+    x_hbm, step_hbm, decay_hbm, freq_hbm, win_hbm, wout_hbm, skip_hbm, cot_hbm,
     out_ref, ig_ref, gin_ref, gout_ref,
-    xc, wio, xct, stb, lam, drv, pairs, chunk, msg, rmsg, own, theirs, partner,
+    step_ref, decay_ref, freq_ref, skip_ref, xc, wio, xct, stb, lam, drv, pairs, chunk, msg, rmsg, own, theirs, partner,
     r1, r2, up, r3, fin,
-    load_sem, pre_sem, pair_sem, ring_sem, second_sem, z_sem, fin_sem,
+    small_sem, load_sem, pre_sem, pair_sem, ring_sem, second_sem, z_sem, fin_sem,
 ):
     dp = lax.axis_index("dp")
     ctx = lax.axis_index("context")
@@ -68,17 +68,25 @@
         pl.semaphore_signal(barrier, inc=1, device_id=(lax.rem(dp + d, DP), ctx), device_id_type=MESH)
         return 0
 
+    small = [
+        pltpu.make_async_copy(src, dst, small_sem.at[k])
+        for k, (src, dst) in enumerate(
+            ((step_hbm, step_ref), (decay_hbm, decay_ref), (freq_hbm, freq_ref), (skip_hbm, skip_ref))
+        )
+    ]
     loads = [
         pltpu.make_async_copy(x_hbm, xc.at[0], load_sem.at[0]),
         pltpu.make_async_copy(win_hbm, wio.at[0], load_sem.at[1]),
         pltpu.make_async_copy(cot_hbm, xc.at[1], load_sem.at[2]),
         pltpu.make_async_copy(wout_hbm, wio.at[1], load_sem.at[3]),
     ]
-    for load in loads:
+    for load in small + loads:
         load.start()
     lax.fori_loop(1, PEERS, greet_context, 0)
     lax.fori_loop(1, DP, greet_dp, 0)
 
+    for load in small:
+        load.wait()
     decay = [decay_ref[:, g * 128 : (g + 1) * 128] for g in range(2)]
     freq = [freq_ref[:, g * 128 : (g + 1) * 128] for g in range(2)]
     gain = []
@@ -139,7 +147,7 @@
         return (*nf, *nb, total)
 
     zero = jnp.zeros((SUB, 128), F32)
-    summary = lax.fori_loop(0, LAPS, lambda j, c: scan_step(j, c, False), (zero,) * 9)
+    summary = lax.fori_loop(0, LAPS, lambda j, c: scan_step(j, c, False), (zero,) * 9, unroll=4)
     for k in range(8):
         chunk[4 + k] = summary[k]
     for g in range(2):
@@ -179,7 +187,7 @@
             if dz or dy:
                 peer = lax.rem(z + dz, NZ) * NY + lax.rem(y + dy, NY)
                 pltpu.make_async_remote_copy(
-                    src_ref=msg.at[(peer < ctx).astype(jnp.int32)], dst_ref=rmsg.at[ctx],
+                    src_ref=msg.at[(peer < ctx).astype(jnp.int32), pl.ds(0, 5)], dst_ref=rmsg.at[ctx, pl.ds(0, 5)],
                     send_sem=pre_sem.at[0], recv_sem=pre_sem.at[1],
                     device_id=(dp, peer), device_id_type=MESH,
                 ).start()
@@ -193,7 +201,7 @@
         lax.fori_loop(0, WIDTH // 128, turn_block, 0)
 
     everyone = pltpu.make_async_remote_copy(
-        src_ref=rmsg.at[pl.ds(0, PEERS - 1)], dst_ref=rmsg.at[pl.ds(0, PEERS - 1)],
+        src_ref=rmsg.at[pl.ds(0, PEERS - 1), pl.ds(0, 5)], dst_ref=rmsg.at[pl.ds(0, PEERS - 1), pl.ds(0, 5)],
         send_sem=pre_sem.at[0], recv_sem=pre_sem.at[1],
         device_id=(dp, lax.rem(ctx + 1, PEERS)), device_id_type=MESH,
     )
@@ -216,7 +224,7 @@
             entering[4 + h] = jnp.sum(jnp.where(place > ctx, v, 0.0), axis=0, keepdims=True)
     pass_chunks(entering, True)
     start = tuple(chunk[12 + k] for k in range(8)) + (zero,)
-    lax.fori_loop(0, LAPS, lambda j, c: scan_step(j, c, True), start)
+    lax.fori_loop(0, LAPS, lambda j, c: scan_step(j, c, True), start, unroll=4)
 
     def round_block(i, _):
         rows = pl.ds(pl.multiple_of(i * 32, 32), 32)
@@ -360,18 +368,18 @@
     out_block(1, 0)
     relay(0)
     begin(3)
+    relay(1)
     out_block(1, 1)
-    relay(1)
+    relay(2)
+    out_block(1, 2)
     turn_corner(0)
-    out_block(1, 2)
-    relay(2)
+    relay(3)
+    out_block(1, 3)
     turn_corner(1)
+    turn_corner(2)
     climb(0)
-    out_block(1, 3)
-    relay(3)
-    turn_corner(2)
+    turn_corner(3)
     climb(1)
-    turn_corner(3)
     climb(2)
     climb(3)
 
@@ -425,9 +433,13 @@
     held = pl.pallas_call(
         kernel,
         out_shape=tuple(pltpu.VMEM(shape, dtype) for shape, dtype in results),
-        in_specs=[hbm, vmem, vmem, vmem, hbm, hbm, vmem, hbm],
+        in_specs=[hbm] * 8,
         out_specs=(vmem,) * 4,
         scratch_shapes=[
+            pltpu.VMEM((1, ROWS), F32),
+            pltpu.VMEM((1, STATES), F32),
+            pltpu.VMEM((1, STATES), F32),
+            pltpu.VMEM((1, WIDTH), F32),
             pltpu.VMEM((2, ROWS, WIDTH), BF16),
             pltpu.VMEM((2, WIDTH, 2 * STATES), BF16),
             pltpu.VMEM((2, WIDTH, ROWS), BF16),
@@ -447,6 +459,7 @@
             pltpu.VMEM((NZ, 32, 128), F32),
             pltpu.VMEM((DP, 32, 128), F32),
             pltpu.SemaphoreType.DMA((4,)),
+            pltpu.SemaphoreType.DMA((4,)),
             pltpu.SemaphoreType.DMA((2,)),
             pltpu.SemaphoreType.DMA((2, PARTS)),
             pltpu.SemaphoreType.DMA((2, PARTS, 6)),

time: 48.6 us -> 45.1 us (0.928)
  Pallas kernels: 47.8 us -> 44.4 us
    pallas_call x1, Pallas kernels: 46.4 us -> 43 us  [on_device(): pl.pallas_call(kernel, out_shape=tuple((pltpu.VMEM(shape, dtype) for shap...]
where the time goes in v4:
time: 45.1 us; the launch traced here: 45 us
  Pallas kernels  44.4 us (98%)
  between operations  0.64 us (1%)
    pallas_call x1, Pallas kernels, on_device(): pl.pallas_call(kernel, out_shape=tuple((pltpu.VMEM(shape, dtype) for shap...  43 us
    pallas_call x1, Pallas kernels, on_device(): pl.pallas_call(store_kernel, out_shape=tuple((jax.ShapeDtypeStruct(shape,...  1.38 us

profile of v4, /device:TPU:1, one launch (start us, length us, event | category | flops | bytes accessed | tf_op | source)
XLA Modules:
  0.0 45.0 jit_solution(8807199516123425663)
XLA Ops:
  0.6 43.0 %shard_map.111 = (bf16[512,1024]{1,0:T(8,128)(2,1)S(1)}, bf16[512,1024]{1,0:T(8,128)(2,1)S(1)}, f32[32,512]{1,0:T(8,128)S(1)}, f32[32,512]{1,0:T(8,128)S(1)}) custom-call(bf16[512,1024]{1,0:T(8,128)(2,1)} %bitcast.7, f32[1,512]{1,0:T(1,128)} %step_hbm.1, f32[1,256]{1,0:T(1,128)} %bitcast.10, f32[1,256]{1,0:T(1,128)} %bitcast.11, bf16[1024,512]{1,0:T(8,128)(2,1)} %win_hbm.1, ...), custom_call_target="tpu_custom_call" | custom-call | tf_op jit(solution)/shard_map/pallas_call | solution.py:433
  43.7 1.4 %shard_map.112 = (bf16[512,1024]{1,0:T(8,128)(2,1)}, bf16[512,1024]{1,0:T(8,128)(2,1)}, f32[32,512]{1,0:T(8,128)}, f32[32,512]{1,0:T(8,128)}) custom-call(bf16[512,1024]{1,0:T(8,128)(2,1)S(1)} %get-tuple-element.12.refs_0_, bf16[512,1024]{1,0:T(8,128)(2,1)S(1)} %get-tuple-element.13.refs_1_, f32[32,512]{1,0:T(8,128)S(1)} %get-tuple-element.14.refs_2_, ...), custom_call_target="tpu_custom_call" | custom-call | tf_op jit(solution)/shard_map/pallas_call | solution.py:477

commit v5 on v4

--- a/solution.py
+++ b/solution.py
@@ -154,15 +154,14 @@
         chunk[g], chunk[2 + g] = turn(jnp.minimum(summary[8], 8.0e6), decay[g], freq[g])
     msg[...] = jnp.zeros_like(msg)
 
-    def pass_chunks(entering, keep):
-        f, b = list(entering[:4]), list(entering[4:])
+    def pass_chunks():
+        f, b = [jnp.zeros((1, 128), F32)] * 4, [jnp.zeros((1, 128), F32)] * 4
         for s in range(SUB):
             e = SUB - 1 - s
             for g in range(2):
-                if keep:
-                    for h in (g, 2 + g):
-                        chunk[12 + h, s : s + 1, :] = f[h]
-                        chunk[16 + h, e : e + 1, :] = b[h]
+                for h in (g, 2 + g):
+                    chunk[12 + h, s : s + 1, :] = f[h]
+                    chunk[16 + h, e : e + 1, :] = b[h]
                 re, im = cmul(chunk[g, s : s + 1, :], chunk[2 + g, s : s + 1, :], f[g], f[2 + g])
                 f[g] = re + chunk[4 + g, s : s + 1, :]
                 f[2 + g] = im + chunk[6 + g, s : s + 1, :]
@@ -171,7 +170,7 @@
                 b[2 + g] = im + chunk[10 + g, e : e + 1, :]
         return f + b
 
-    leave = pass_chunks((jnp.zeros((1, 128), F32),) * 8, False)
+    leave = pass_chunks()
     total = jnp.sum(summary[8], axis=0, keepdims=True)
     for k in range(4):
         msg[0, k : k + 1, :] = leave[k]
@@ -191,6 +190,15 @@
                     send_sem=pre_sem.at[0], recv_sem=pre_sem.at[1],
                     device_id=(dp, peer), device_id_type=MESH,
                 ).start()
+
+    line = lax.broadcasted_iota(jnp.int32, (SUB, 128), 0)
+    ahead = behind = jnp.zeros((SUB, 128), F32)
+    for s in range(SUB):
+        ahead = ahead + jnp.where(line > s, summary[8][s : s + 1], 0.0)
+        behind = behind + jnp.where(line < s, summary[8][s : s + 1], 0.0)
+    for g in range(2):
+        chunk[20 + g], chunk[22 + g] = turn(jnp.minimum(ahead, 8.0e6), decay[g], freq[g])
+        chunk[24 + g], chunk[26 + g] = turn(jnp.minimum(behind, 8.0e6), decay[g], freq[g])
 
     for m in range(2):
         def turn_block(i, _, m=m):
@@ -222,8 +230,13 @@
         for h, v in ((g, re), (2 + g, im)):
             entering[h] = jnp.sum(jnp.where(place < ctx, v, 0.0), axis=0, keepdims=True)
             entering[4 + h] = jnp.sum(jnp.where(place > ctx, v, 0.0), axis=0, keepdims=True)
-    pass_chunks(entering, True)
-    start = tuple(chunk[12 + k] for k in range(8)) + (zero,)
+    start = [None] * 8
+    for g in range(2):
+        re, im = cmul(chunk[20 + g], chunk[22 + g], entering[g], entering[2 + g])
+        start[g], start[2 + g] = chunk[12 + g] + re, chunk[14 + g] + im
+        re, im = cmulc(chunk[24 + g], chunk[26 + g], entering[4 + g], entering[6 + g])
+        start[4 + g], start[6 + g] = chunk[16 + g] + re, chunk[18 + g] + im
+    start = (*start, zero)
     lax.fori_loop(0, LAPS, lambda j, c: scan_step(j, c, True), start, unroll=4)
 
     def round_block(i, _):
@@ -236,22 +249,15 @@
 
     lax.fori_loop(0, ROWS // 32, round_block, 0)
 
-    def gradient(m, into, then=None):
-        def rows_block(i, _):
-            rows = pl.ds(pl.multiple_of(i * 256, 256), 256)
-            res = jnp.dot(xct[m, rows, :], pairs[m], preferred_element_type=F32)
-            for zi in range(2):
-                for yy in range(NY):
-                    top = (zi * NY + yy) * 32
-                    for q in range(NX):
-                        a = q + m * (yy - q)
-                        b = yy + m * (q - yy)
-                        into[i, a, b, zi] = res[top : top + 32, q * 128 : (q + 1) * 128]
-            if then is not None:
-                then(i)
-            return 0
-
-        lax.fori_loop(0, PARTS, rows_block, 0)
+    def gradient(m, into, block):
+        res = jnp.dot(xct[m, block * 512 : (block + 1) * 512, :], pairs[m], preferred_element_type=F32)
+        for zi in range(4):
+            for yy in range(NY):
+                top = (zi * NY + yy) * 32
+                for q in range(NX):
+                    a = q + m * (yy - q)
+                    b = yy + m * (q - yy)
+                    into[2 * block + zi // 2, a, b, zi % 2] = res[top : top + 32, q * 128 : (q + 1) * 128]
 
     spot = x + core * (y - x)
     spot_other = y + core * (x - y)
@@ -263,8 +269,12 @@
             device_id=(2 * x + other, ctx), device_id_type=MESH,
         )
 
-    gradient(other, theirs, lambda i: swap(i).start())
-    gradient(core, own)
+    for block in range(2):
+        gradient(other, theirs, block)
+        swap(2 * block).start()
+        swap(2 * block + 1).start()
+    for block in range(2):
+        gradient(core, own, block)
 
     def first_ring(d):
         return (2 * lax.rem(x + other * d, 4) + core, z * NY + lax.rem(y + core * d, 4))
@@ -447,7 +457,7 @@
             pltpu.VMEM((4, SUB * PITCH, 128), F32),
             pltpu.VMEM((2, 4, SUB * PITCH, 128), F32),
             pltpu.VMEM((2, ROWS, 2 * STATES), BF16),
-            pltpu.VMEM((20, SUB, 128), F32),
+            pltpu.VMEM((28, SUB, 128), F32),
             pltpu.VMEM((2, 8, 128), F32),
             pltpu.VMEM((PEERS, 8, 128), F32),
             pltpu.VMEM((PARTS, 4, 4, 2, 32, 128), F32),

time: 45.1 us -> 44.3 us (0.982)
  Pallas kernels: 44.4 us -> 43.6 us
    pallas_call x1, Pallas kernels: 43 us -> 42.2 us  [on_device(): pl.pallas_call(kernel, out_shape=tuple((pltpu.VMEM(shape, dtype) for shap...]
where the time goes in v5:
time: 44.3 us; the launch traced here: 44.2 us
  Pallas kernels  43.6 us (98%)
  between operations  0.64 us (1%)
    pallas_call x1, Pallas kernels, on_device(): pl.pallas_call(kernel, out_shape=tuple((pltpu.VMEM(shape, dtype) for shap...  42.2 us
    pallas_call x1, Pallas kernels, on_device(): pl.pallas_call(store_kernel, out_shape=tuple((jax.ShapeDtypeStruct(shape,...  1.38 us

profile of v5, /device:TPU:1, one launch (start us, length us, event | category | flops | bytes accessed | tf_op | source)
XLA Modules:
  0.0 44.2 jit_solution(9733875579014579237)
XLA Ops:
  0.6 42.2 %shard_map.111 = (bf16[512,1024]{1,0:T(8,128)(2,1)S(1)}, bf16[512,1024]{1,0:T(8,128)(2,1)S(1)}, f32[32,512]{1,0:T(8,128)S(1)}, f32[32,512]{1,0:T(8,128)S(1)}) custom-call(bf16[512,1024]{1,0:T(8,128)(2,1)} %bitcast.7, f32[1,512]{1,0:T(1,128)} %step_hbm.1, f32[1,256]{1,0:T(1,128)} %bitcast.10, f32[1,256]{1,0:T(1,128)} %bitcast.11, bf16[1024,512]{1,0:T(8,128)(2,1)} %win_hbm.1, ...), custom_call_target="tpu_custom_call" | custom-call | tf_op jit(solution)/shard_map/pallas_call | solution.py:443
  42.8 1.4 %shard_map.112 = (bf16[512,1024]{1,0:T(8,128)(2,1)}, bf16[512,1024]{1,0:T(8,128)(2,1)}, f32[32,512]{1,0:T(8,128)}, f32[32,512]{1,0:T(8,128)}) custom-call(bf16[512,1024]{1,0:T(8,128)(2,1)S(1)} %get-tuple-element.12.refs_0_, bf16[512,1024]{1,0:T(8,128)(2,1)S(1)} %get-tuple-element.13.refs_1_, f32[32,512]{1,0:T(8,128)S(1)} %get-tuple-element.14.refs_2_, ...), custom_call_target="tpu_custom_call" | custom-call | tf_op jit(solution)/shard_map/pallas_call | solution.py:487

commit v6 on v5

--- a/solution.py
+++ b/solution.py
@@ -50,7 +50,7 @@
     out_ref, ig_ref, gin_ref, gout_ref,
     step_ref, decay_ref, freq_ref, skip_ref, xc, wio, xct, stb, lam, drv, pairs, chunk, msg, rmsg, own, theirs, partner,
     r1, r2, up, r3, fin,
-    small_sem, load_sem, pre_sem, pair_sem, ring_sem, second_sem, z_sem, fin_sem,
+    small_sem, load_sem, pre_sem, quarter_sem, pair_sem, ring_sem, second_sem, z_sem, fin_sem,
 ):
     dp = lax.axis_index("dp")
     ctx = lax.axis_index("context")
@@ -103,16 +103,13 @@
         for s in (0, 1):
             stb[pl.ds((2 * r + s) * PITCH, LAPS), :] = turned[s * LAPS : (s + 1) * LAPS]
 
-    def lam_block(i, _):
-        rows = pl.ds(lax.div(i, 2) * PITCH + lax.rem(i, 2) * 32, 32)
+    def lam_block(i):
+        rows = pl.ds((i // 2) * PITCH + (i % 2) * 32, 32)
         st = stb[rows, :]
         for g in range(2):
             re, im = turn(st, decay[g], freq[g])
             lam[g, rows, :] = re
             lam[2 + g, rows, :] = im
-        return 0
-
-    lax.fori_loop(0, ROWS // 32, lam_block, 0)
 
     for m in range(2):
         loads[2 * m].wait()
@@ -124,6 +121,8 @@
                 part = part * gain[g] if m == 0 else part
                 for s in range(SUB):
                     drv[m, 2 * nb + g, s * PITCH : s * PITCH + LAPS, :] = part[s * LAPS : (s + 1) * LAPS]
+            for i in range(4):
+                lam_block(8 * m + 4 * nb + i)
 
     def scan_step(j, carry, store):
         f, b, total = carry[:4], carry[4:8], carry[8]
@@ -239,15 +238,17 @@
     start = (*start, zero)
     lax.fori_loop(0, LAPS, lambda j, c: scan_step(j, c, True), start, unroll=4)
 
-    def round_block(i, _):
-        rows = pl.ds(pl.multiple_of(i * 32, 32), 32)
-        held = pl.ds(lax.div(i, 2) * PITCH + lax.rem(i, 2) * 32, 32)
-        for k in range(4):
-            pairs[0, rows, k * 128 : (k + 1) * 128] = (drv[1, k, held, :] * gain[k % 2]).astype(BF16)
-            pairs[1, rows, k * 128 : (k + 1) * 128] = drv[0, k, held, :].astype(BF16)
-        return 0
-
-    lax.fori_loop(0, ROWS // 32, round_block, 0)
+    def round_pairs(w):
+        scale = [jnp.where(w == 0, gain[g], 1.0) for g in range(2)]
+
+        def round_block(i, _):
+            rows = pl.ds(pl.multiple_of(i * 64, 64), 64)
+            held = pl.ds(i * PITCH, 64)
+            for k in range(4):
+                pairs[w, rows, k * 128 : (k + 1) * 128] = (drv[1 - w, k, held, :] * scale[k % 2]).astype(BF16)
+            return 0
+
+        lax.fori_loop(0, SUB, round_block, 0)
 
     def gradient(m, into, block):
         res = jnp.dot(xct[m, block * 512 : (block + 1) * 512, :], pairs[m], preferred_element_type=F32)
@@ -269,10 +270,24 @@
             device_id=(2 * x + other, ctx), device_id_type=MESH,
         )
 
-    for block in range(2):
-        gradient(other, theirs, block)
-        swap(2 * block).start()
-        swap(2 * block + 1).start()
+    def swap_quarter(k, theirs_place=None):
+        place = spot_other if theirs_place is None else theirs_place
+        a = lax.rem(place + (2, 1, 3, 0)[k], 4)
+        return pltpu.make_async_remote_copy(
+            src_ref=theirs.at[0, a], dst_ref=partner.at[0, a],
+            send_sem=quarter_sem.at[0, k], recv_sem=quarter_sem.at[1, k],
+            device_id=(2 * x + other, ctx), device_id_type=MESH,
+        )
+
+    round_pairs(other)
+    gradient(other, theirs, 0)
+    for k in range(4):
+        swap_quarter(k).start()
+    swap(1).start()
+    gradient(other, theirs, 1)
+    swap(2).start()
+    swap(3).start()
+    round_pairs(core)
     for block in range(2):
         gradient(core, own, block)
 
@@ -306,17 +321,20 @@
     seconds = [None] * PARTS
 
     def begin(i):
-        swap(i).wait_recv()
-
-        def add(a, _):
+        if i > 0:
+            swap(i).wait_recv()
+        for k, d in enumerate((2, 1, 3, 0)):
+            if i == 0:
+                swap_quarter(k, spot).wait_recv()
+            a = lax.rem(spot + d, 4)
             own[i, a] += partner[i, a]
-            return 0
-
-        lax.fori_loop(0, 4, add, 0)
-        firsts[i][0] = send_first(i, 0, half(i, 2, 0), 1)
-        firsts[i][1] = send_first(i, 1, half(i, 2, 1), 3)
-        firsts[i][2] = send_first(i, 2, half(i, 1, 1), 1)
-        firsts[i][3] = send_first(i, 3, half(i, 3, 0), 3)
+            if k == 0:
+                firsts[i][0] = send_first(i, 0, half(i, 2, 0), 1)
+                firsts[i][1] = send_first(i, 1, half(i, 2, 1), 3)
+            elif k == 1:
+                firsts[i][2] = send_first(i, 2, half(i, 1, 1), 1)
+            elif k == 2:
+                firsts[i][3] = send_first(i, 3, half(i, 3, 0), 3)
 
     def relay(i):
         firsts[i][0].wait_recv()
@@ -416,7 +434,9 @@
         device_id=(lax.rem(dp + 1, DP), ctx), device_id_type=MESH,
     )
     column.wait_send()
-    for i in range(PARTS):
+    for k in range(4):
+        swap_quarter(k).wait_send()
+    for i in range(1, PARTS):
         swap(i).wait_send()
     for copy in sent:
         copy.wait_send()
@@ -471,6 +491,7 @@
             pltpu.SemaphoreType.DMA((4,)),
             pltpu.SemaphoreType.DMA((4,)),
             pltpu.SemaphoreType.DMA((2,)),
+            pltpu.SemaphoreType.DMA((2, 4)),
             pltpu.SemaphoreType.DMA((2, PARTS)),
             pltpu.SemaphoreType.DMA((2, PARTS, 6)),
             pltpu.SemaphoreType.DMA((2, PARTS, 3)),

time: 44.3 us -> 44.2 us (level)
  no operation moved by 1% of the time
where the time goes in v6:
time: 44.2 us; the launch traced here: 44.1 us
  Pallas kernels  43.4 us (98%)
  between operations  0.64 us (1%)
    pallas_call x1, Pallas kernels, on_device(): pl.pallas_call(kernel, out_shape=tuple((pltpu.VMEM(shape, dtype) for shap...  42.1 us
    pallas_call x1, Pallas kernels, on_device(): pl.pallas_call(store_kernel, out_shape=tuple((jax.ShapeDtypeStruct(shape,...  1.38 us

profile of v6, /device:TPU:1, one launch (start us, length us, event | category | flops | bytes accessed | tf_op | source)
XLA Modules:
  0.0 44.1 jit_solution(5485245356546217917)
XLA Ops:
  0.6 42.1 %shard_map.111 = (bf16[512,1024]{1,0:T(8,128)(2,1)S(1)}, bf16[512,1024]{1,0:T(8,128)(2,1)S(1)}, f32[32,512]{1,0:T(8,128)S(1)}, f32[32,512]{1,0:T(8,128)S(1)}) custom-call(bf16[512,1024]{1,0:T(8,128)(2,1)} %bitcast.7, f32[1,512]{1,0:T(1,128)} %step_hbm.1, f32[1,256]{1,0:T(1,128)} %bitcast.10, f32[1,256]{1,0:T(1,128)} %bitcast.11, bf16[1024,512]{1,0:T(8,128)(2,1)} %win_hbm.1, ...), custom_call_target="tpu_custom_call" | custom-call | tf_op jit(solution)/shard_map/pallas_call | solution.py:463
  42.7 1.4 %shard_map.112 = (bf16[512,1024]{1,0:T(8,128)(2,1)}, bf16[512,1024]{1,0:T(8,128)(2,1)}, f32[32,512]{1,0:T(8,128)}, f32[32,512]{1,0:T(8,128)}) custom-call(bf16[512,1024]{1,0:T(8,128)(2,1)S(1)} %get-tuple-element.12.refs_0_, bf16[512,1024]{1,0:T(8,128)(2,1)S(1)} %get-tuple-element.13.refs_1_, f32[32,512]{1,0:T(8,128)S(1)} %get-tuple-element.14.refs_2_, ...), custom_call_target="tpu_custom_call" | custom-call | tf_op jit(solution)/shard_map/pallas_call | solution.py:508
